TPU v7x, 32 devices: a whole 2x2x4 slice. The times are simulated.
32 devices in a mesh: dp: 8 (over y, x, core), tensor: 4 (over z).
Axes of the slice: x: 2, y: 2, z: 4, core: 2. Of those that a mesh axis runs over, the one named last changes fastest.
Arguments:
- inputs: bfloat16 [32768, 768], P('dp'), may hold values from -6 to 6
- segments: int32 [64, 512], P('dp'), may hold values from 0 to 7, never falling along the last dimension, each value on 1 to 128 neighbouring positions
- w_query: bfloat16 [768, 768], P(None, 'tensor'), may hold values from -0.21875 to 0.21875
- w_key: bfloat16 [768, 768], P(None, 'tensor'), may hold values from -0.21875 to 0.21875
- w_value: bfloat16 [768, 768], P(None, 'tensor'), may hold values from -0.21875 to 0.21875
- b_query: bfloat16 [768], P('tensor'), may hold values from -3 to 3
- b_value: bfloat16 [768], P('tensor'), may hold values from -3 to 3
- w_output: bfloat16 [768, 768], P('tensor'), may hold values from -0.875 to 0.875
- b_output: bfloat16 [768], replicated, may hold values from -3 to 3
- gain_attn: bfloat16 [768], replicated, may hold values from 0.5 to 1.5
- shift_attn: bfloat16 [768], replicated, may hold values from -3 to 3
- w_hidden: bfloat16 [768, 3072], P(None, 'tensor'), may hold values from -0.21875 to 0.21875
- b_hidden: bfloat16 [3072], P('tensor'), may hold values from -3 to 3
- w_project: bfloat16 [3072, 768], P('tensor'), may hold values from -0.109375 to 0.109375
- b_project: bfloat16 [768], replicated, may hold values from -3 to 3
- gain_ffn: bfloat16 [768], replicated, may hold values from 0.5 to 1.5
- shift_ffn: bfloat16 [768], replicated, may hold values from -3 to 3
- cotangent: bfloat16 [32768, 768], P(('dp', 'tensor')), may hold values from -6 to 6
Outputs:
- output: bfloat16 [32768, 768], P(('dp', 'tensor'))
- grad_input: float32 [32768, 768], P(('dp', 'tensor'))
- grad_w_query: float32 [768, 768], P('dp', 'tensor')
- grad_w_key: float32 [768, 768], P('dp', 'tensor')
- grad_w_value: float32 [768, 768], P('dp', 'tensor')
- grad_w_output: float32 [768, 768], P('tensor', 'dp')
- grad_w_hidden: float32 [768, 3072], P('dp', 'tensor')
- grad_w_project: float32 [3072, 768], P('tensor', 'dp')
- grad_bias_qv: float32 [2, 12, 64], P(None, 'tensor', 'dp')
- grad_b_hidden: float32 [48, 64], P('tensor', 'dp')
- grad_vectors: float32 [6, 768], P(None, ('dp', 'tensor'))
Inputs may be any that keep to these rules, and one draw needn't show every extreme that they name: `segments`: within each row of 512 tokens segment numbers never fall; each text holds 1 to 128 tokens, and some text holds exactly 128.
All inputs are finite; a program needn't handle non-finite values.
Results may differ from a plain program's by a relative error of at most 0.014.
Values may be sent and summed in bfloat16 or wider, within the bound.
A program may use at most 192 MiB of HBM per device.

v0:
```python
import functools
import jax
import jax.numpy as jnp
from jax import lax
from jax.experimental import pallas as pl
from jax.experimental.pallas import tpu as pltpu
from jax.sharding import PartitionSpec as P

HD = 64
MESH = pl.DeviceIdType.MESH
LOW = jnp.bfloat16


class Place:
    def __init__(self, groups, parts):
        self.groups, self.parts = groups, parts
        self.t, self.d = lax.axis_index("tensor"), lax.axis_index("dp")
        self.count = parts.bit_length() - 1
        self.bits = [(self.d // (1 << i)) % 2 for i in range(self.count)]

    def partner(self, bit):
        return (self.d + (1 - 2 * self.bits[bit]) * (1 << bit), self.t)

    def along(self, step):
        return (self.d, (self.t + step) % self.groups)

    def enter(self):
        barrier = pltpu.get_barrier_semaphore()
        peers = [self.partner(b) for b in range(self.count)]
        peers += [self.along(j) for j in range(1, self.groups)]
        for peer in peers:
            pl.semaphore_signal(barrier, inc=1, device_id=peer, device_id_type=MESH)
        pl.semaphore_wait(barrier, len(peers))

    def pieces(self, open_bits, flipped=None):
        index = []
        for bit in reversed(range(self.count)):
            own = self.bits[bit]
            index.append(slice(None) if bit in open_bits else 1 - own if bit == flipped else own)
        return tuple(index)


def send(src, dst, sems, slot, peer):
    return pltpu.make_async_remote_copy(
        src_ref=src,
        dst_ref=dst,
        send_sem=sems[0].at[slot],
        recv_sem=sems[1].at[slot],
        device_id=peer,
        device_id_type=MESH,
    )


def orders(count):
    rest = list(range(1, count))
    return [rest, rest[::-1]]


def gather_kernel(groups, parts, arrays, *refs):
    shards, small = refs[:arrays], refs[arrays]
    outs, small_out = refs[arrays + 1 : 2 * arrays + 1], refs[2 * arrays + 1]
    held, small_held = refs[2 * arrays + 2 : 3 * arrays + 2], refs[3 * arrays + 2]
    load_sem, store_sem, z_send, z_recv, x_send, x_recv, s_send, s_recv = refs[3 * arrays + 3 :]
    me = Place(groups, parts)
    n = me.count
    half = shards[0].shape[-1] // 2
    bits_order = orders(n)
    me.enter()
    own = [me.t] + list(me.pieces(()))
    hops, doubles, tiny = {}, {}, []
    for j in range(1, groups):
        tiny.append(send(small, small_held.at[j - 1], (s_send, s_recv), j - 1, me.along(j)))
        tiny[-1].start()
    for a in range(arrays):
        for j in range(1, groups):
            u = a * (groups - 1) + j - 1
            hops[u] = send(
                shards[a].at[tuple(me.pieces(()))], held[a].at[tuple(own)], (z_send, z_recv), u, me.along(j)
            )
            hops[u].start()
    loads = []
    for a in range(arrays):
        loads.append(pltpu.make_async_copy(shards[a], held[a].at[me.t], load_sem.at[a]))
        loads[-1].start()

    units = arrays * (groups - 1)
    stores = []

    def advance(u, stage):
        a, j = divmod(u, groups - 1)
        source = (me.t + groups - 1 - j) % groups
        if stage == 0:
            hops[u].wait_recv()
        else:
            for h in range(2):
                if stage < n or h == 0:
                    doubles[u, stage - 1, h].wait_recv()
        if stage == n:
            out = pltpu.make_async_copy(held[a].at[source], outs[a].at[source], store_sem.at[u])
            out.start()
            stores.append(out)
            return
        for h in range(2):
            if stage == n - 1:
                if h == 1:
                    continue
                bit, done, cols = 0, set(range(1, n)), slice(None)
            else:
                bit, done = bits_order[h][stage], set(bits_order[h][:stage])
                cols = pl.ds(h * half, half)
            view = (source,) + me.pieces(done) + (slice(None), cols)
            slot = (u * n + stage) * 2 + h
            copy = send(held[a].at[view], held[a].at[view], (x_send, x_recv), slot, me.partner(bit))
            copy.start()
            doubles[u, stage, h] = copy

    for tick in range(units + n):
        for stage in range(n + 1):
            u = tick - stage
            if 0 <= u < units:
                advance(u, stage)
    for a in range(arrays):
        loads[a].wait()
        out = pltpu.make_async_copy(held[a].at[me.t], outs[a].at[me.t], store_sem.at[units + a])
        out.start()
        stores.append(out)
    small_out[me.t] = small[...]
    for j in range(1, groups):
        tiny[j - 1].wait()
        small_out[(me.t + groups - j) % groups] = small_held[j - 1]
    for copy in hops.values():
        copy.wait_send()
    for copy in doubles.values():
        copy.wait_send()
    for copy in stores:
        copy.wait()


def gather(shards, small, groups, parts):
    arrays, n = len(shards), parts.bit_length() - 1
    rows, cols = shards[0].shape[0] // parts, shards[0].shape[1]
    shape = (2,) * n + (rows, cols)
    units = arrays * (groups - 1)
    any_space = pl.BlockSpec(memory_space=pl.ANY)
    vmem = pl.BlockSpec(memory_space=pltpu.VMEM)
    *outs, small = pl.pallas_call(
        functools.partial(gather_kernel, groups, parts, arrays),
        out_shape=[jax.ShapeDtypeStruct((groups,) + shape, LOW)] * arrays
        + [jax.ShapeDtypeStruct((groups,) + small.shape, LOW)],
        in_specs=[any_space] * arrays + [vmem],
        out_specs=[any_space] * arrays + [vmem],
        scratch_shapes=[pltpu.VMEM((groups,) + shape, LOW)] * arrays
        + [
            pltpu.VMEM((groups - 1,) + small.shape, LOW),
            pltpu.SemaphoreType.DMA((arrays,)),
            pltpu.SemaphoreType.DMA((units + arrays,)),
            pltpu.SemaphoreType.DMA((units,)),
            pltpu.SemaphoreType.DMA((units,)),
            pltpu.SemaphoreType.DMA((units * n * 2,)),
            pltpu.SemaphoreType.DMA((units * n * 2,)),
            pltpu.SemaphoreType.DMA((groups - 1,)),
            pltpu.SemaphoreType.DMA((groups - 1,)),
        ],
        compiler_params=pltpu.CompilerParams(
            collective_id=0, has_side_effects=True, vmem_limit_bytes=60 << 20
        ),
        name="gather_weights",
    )(*[s.reshape(shape) for s in shards], small)
    return [o.reshape(groups, parts * rows, cols) for o in outs], small


def add_into(dst, src, lead):
    def one(i, carry):
        index = []
        for size in reversed(lead):
            index.append(i % size)
            i = i // size
        index = tuple(reversed(index))
        total = dst[index].astype(jnp.float32) + src[index].astype(jnp.float32)
        dst[index] = total.astype(LOW)
        return carry

    total = 1
    for size in lead:
        total *= size
    lax.fori_loop(0, total, one, 0)


def scatter_kernel(groups, parts, arrays, *refs):
    parted, vec = refs[:arrays], refs[arrays]
    outs, vec_out = refs[arrays + 1 : 2 * arrays + 1], refs[2 * arrays + 1]
    p = 2 * arrays + 2
    held = refs[p : p + arrays]
    n = parts.bit_length() - 1
    p += arrays
    landing = refs[p]
    halves = refs[p + 1 : p + n]
    final = refs[p + n]
    load_sem, x_send, x_recv, z_send, z_recv, vec_sum, vec_land, v_send, v_recv = refs[p + n + 1 :]
    me = Place(groups, parts)
    half = parted[0].shape[-1] // 2
    bits_order = orders(n)
    units = arrays * groups
    loads = []
    turn = [(u // groups, (me.t + 1 + u % groups) % groups) for u in range(units)]
    for u in range(units):
        a, target = turn[u]
        copy = pltpu.make_async_copy(parted[a].at[target], held[a].at[target], load_sem.at[u])
        copy.start()
        loads.append(copy)
    me.enter()
    copies, hops, tiny = {}, {}, {}

    def advance_vectors(stage):
        source = vec if stage == 0 else vec_sum.at[stage - 1]
        if stage:
            tiny[stage - 1].wait_recv()
            before = vec[...] if stage == 1 else vec_sum[stage - 2]
            vec_sum[stage - 1] = before + vec_land[stage - 1]
        peers = [me.partner(stage)] if stage < n else [me.along(j) for j in range(1, groups)]
        for k, peer in enumerate(peers):
            copy = send(source, vec_land.at[stage + k], (v_send, v_recv), stage + k, peer)
            copy.start()
            tiny[stage + k] = copy

    def advance(u, stage):
        a, target = turn[u]
        if stage == 0:
            loads[u].wait()
            copy = send(
                held[a].at[(target,) + me.pieces(set(range(1, n)), 0)],
                landing.at[u],
                (x_send, x_recv),
                u * 2 * n,
                me.partner(0),
            )
            copy.start()
            copies[u, 0, 0] = copy
            return
        for h in range(2):
            if stage == 1:
                if h == 1:
                    continue
                left, cols, source = set(range(1, n)), slice(None), landing.at[u]
            else:
                bits = bits_order[h]
                left, cols = set(bits[stage - 1 :]), pl.ds(h * half, half)
                source = halves[stage - 2].at[u, h]
            copies[u, stage - 1, h].wait_recv()
            view = (target,) + me.pieces(left) + (slice(None), cols)
            add_into(held[a].at[view], source, [2] * len(left))
        if stage == n:
            if u % groups < groups - 1:
                j = u % groups + 1
                slot = a * (groups - 1) + j - 1
                hops[slot] = send(
                    held[a].at[(target,) + me.pieces(())], final.at[slot], (z_send, z_recv), slot, me.along(j)
                )
                hops[slot].start()
            return
        for h in range(2):
            bits = bits_order[h]
            bit, left = bits[stage - 1], set(bits[stage:])
            view = (target,) + me.pieces(left, bit) + (slice(None), pl.ds(h * half, half))
            copy = send(
                held[a].at[view],
                halves[stage - 1].at[u, h],
                (x_send, x_recv),
                u * 2 * n + stage * 2 + h,
                me.partner(bit),
            )
            copy.start()
            copies[u, stage, h] = copy

    for tick in range(units + n):
        if tick <= n:
            advance_vectors(tick)
        for stage in reversed(range(n + 1)):
            u = tick - stage
            if 0 <= u < units:
                advance(u, stage)
    total = vec_sum[n - 1]
    for j in range(groups - 1):
        tiny[n + j].wait_recv()
        total = total + vec_land[n + j]
    vec_out[...] = total
    for a in range(arrays):
        total = held[a][(me.t,) + me.pieces(())].astype(jnp.float32)
        for j in range(groups - 1):
            slot = a * (groups - 1) + j
            hops[slot].wait_recv()
            total = total + final[slot].astype(jnp.float32)
        outs[a][...] = total
    for copy in tiny.values():
        copy.wait_send()
    for copy in copies.values():
        copy.wait_send()
    for copy in hops.values():
        copy.wait_send()


def scatter(parted, vec, groups, parts):
    arrays, n = len(parted), parts.bit_length() - 1
    rows, cols = parted[0].shape[1] // parts, parted[0].shape[2]
    shape = (groups,) + (2,) * n + (rows, cols)
    units = arrays * groups
    vmem = pl.BlockSpec(memory_space=pltpu.VMEM)
    return pl.pallas_call(
        functools.partial(scatter_kernel, groups, parts, arrays),
        out_shape=[jax.ShapeDtypeStruct((rows, cols), jnp.float32)] * arrays
        + [jax.ShapeDtypeStruct(vec.shape, jnp.float32)],
        in_specs=[pl.BlockSpec(memory_space=pl.ANY)] * arrays + [vmem],
        out_specs=[vmem] * (arrays + 1),
        scratch_shapes=[pltpu.VMEM(shape, LOW)] * arrays
        + [pltpu.VMEM((units,) + (2,) * (n - 1) + (rows, cols), LOW)]
        + [pltpu.VMEM((units, 2) + (2,) * (n - 1 - s) + (rows, cols // 2), LOW) for s in range(1, n)]
        + [
            pltpu.VMEM((arrays * (groups - 1), rows, cols), LOW),
            pltpu.SemaphoreType.DMA((units,)),
            pltpu.SemaphoreType.DMA((units * 2 * n,)),
            pltpu.SemaphoreType.DMA((units * 2 * n,)),
            pltpu.SemaphoreType.DMA((arrays * (groups - 1),)),
            pltpu.SemaphoreType.DMA((arrays * (groups - 1),)),
            pltpu.VMEM((n,) + vec.shape, jnp.float32),
            pltpu.VMEM((n + groups - 1,) + vec.shape, jnp.float32),
            pltpu.SemaphoreType.DMA((n + groups - 1,)),
            pltpu.SemaphoreType.DMA((n + groups - 1,)),
        ],
        compiler_params=pltpu.CompilerParams(
            collective_id=1, has_side_effects=True, vmem_limit_bytes=60 << 20
        ),
        name="scatter_gradients",
    )(*[g.reshape(shape) for g in parted], vec)


norm_epsilon = 1e-12
root_half = 0.7071067811865476


def norm_forward(values, norm_gain, norm_shift):
    average = jnp.mean(values, axis=-1, keepdims=True)
    centered = values - average
    variance = jnp.mean(centered * centered, axis=-1, keepdims=True)
    inverse = lax.rsqrt(variance + norm_epsilon)
    scaled = centered * inverse
    return (scaled * norm_gain + norm_shift, scaled, inverse)


def norm_backward(grad_out, scaled, inverse, norm_gain):
    weighted = grad_out * norm_gain
    mean_grad = jnp.mean(weighted, axis=-1, keepdims=True)
    mean_proj = jnp.mean(weighted * scaled, axis=-1, keepdims=True)
    return inverse * (weighted - mean_grad - scaled * mean_proj)


def gelu_exact(values):
    return 0.5 * values * (1.0 + lax.erf(values * root_half))


def cross_rows(left, right):
    return lax.dot_general(
        left, right, (((0,), (0,)), ((), ())), preferred_element_type=jnp.float32
    )


def times_transposed(left, right):
    return lax.dot_general(
        left, right, (((1,), (1,)), ((), ())), preferred_element_type=jnp.float32
    )


def masked_scores(queries, keys_in, segment_row):
    same_text = segment_row[:, None] == segment_row[None, :]
    scores = jnp.einsum("qhd,khd->hqk", queries, keys_in, preferred_element_type=jnp.float32)
    scores = scores * queries.shape[2] ** (-0.5)
    return jnp.where(same_text[None], scores, -1000000000.0)


def attend_forward(packed):
    queries, keys_in, values, segment_row = packed
    scores = masked_scores(queries, keys_in, segment_row)
    row_max = jnp.max(scores, axis=-1, keepdims=True)
    exponent = jnp.exp(scores - row_max)
    row_total = jnp.sum(exponent, axis=-1, keepdims=True)
    attn_probs = (exponent / row_total).astype(jnp.bfloat16)
    mixed_heads = jnp.einsum("hqk,khd->qhd", attn_probs, values, preferred_element_type=jnp.float32)
    return (mixed_heads.astype(jnp.bfloat16), row_max + jnp.log(row_total))


def attend_backward(packed):
    queries, keys_in, values, segment_row, logsum, grad_mixed = packed
    score_scale = queries.shape[2] ** (-0.5)
    scores = masked_scores(queries, keys_in, segment_row)
    attn_probs = jnp.exp(scores - logsum)
    grad_probs = jnp.einsum("qhd,khd->hqk", grad_mixed, values, preferred_element_type=jnp.float32)
    grad_values = jnp.einsum(
        "hqk,qhd->khd",
        attn_probs.astype(jnp.bfloat16),
        grad_mixed,
        preferred_element_type=jnp.float32,
    )
    inner_sum = jnp.sum(attn_probs * grad_probs, axis=-1, keepdims=True)
    grad_scores = (attn_probs * (grad_probs - inner_sum)).astype(jnp.bfloat16)
    grad_queries = (
        jnp.einsum("hqk,khd->qhd", grad_scores, keys_in, preferred_element_type=jnp.float32)
        * score_scale
    )
    grad_keys = (
        jnp.einsum("hqk,qhd->khd", grad_scores, queries, preferred_element_type=jnp.float32)
        * score_scale
    )
    return (
        grad_queries.astype(jnp.bfloat16),
        grad_keys.astype(jnp.bfloat16),
        grad_values.astype(jnp.bfloat16),
    )


def matmul_t(left, right):
    return lax.dot_general(left, right, (((1,), (1,)), ((), ())), preferred_element_type=jnp.float32)


TILE = 256
HOP = (10.0, 6.0, 5.0)
PASS = (8.0, 7.0)
SCORE = 1.4426950408889634


def row_tiles(count, size, body, hook=None):
    def step(i, carry):
        body(pl.ds(pl.multiple_of(i * size, size), size))
        if hook:
            hook(i)
        return carry

    lax.fori_loop(0, count // size, step, 0)


class Plan:
    def __init__(self):
        self.now, self.tasks, self.at = 0.0, [], {}

    def add(self, when, task):
        self.tasks.append((when, task))
        self.tasks.sort(key=lambda pair: pair[0])

    def point(self, name, spent, until=None):
        self.now += spent
        if until is not None:
            whens = [when for when, task in self.tasks if task == until]
            if whens:
                self.now = max(self.now, whens[0])
        self.at[name] = [task for when, task in self.tasks if when <= self.now]
        self.tasks = [pair for pair in self.tasks if pair[0] > self.now]


def at_point(plan, run, count, index, name, extra=None):
    for k in range(count):
        tasks = plan.at.get((name, k), [])
        if tasks:
            condition = index == k
            if extra is not None:
                condition = jnp.logical_and(condition, extra)

            @pl.when(condition)
            def _():
                for task in tasks:
                    run(*task)


def key_window(block, blocks, span):
    return max(0, block - 1) * span, min(blocks, block + 2) * span


def fold(values):
    return jnp.sum(values.reshape(-1, 8, values.shape[-1]), axis=0)


def make_mask(mask, seg_col, seg_row):
    def step(r, carry):
        mask[r] = jnp.where(seg_col[r] == seg_row[r], 0.0, -1.0e9)
        return carry

    lax.fori_loop(0, mask.shape[0], step, 0)


def forward_kernel(groups, parts, *refs):
    (first, w_hidden, w_project, inputs, cot_in, small, rows, seg_row, seg_col) = refs[:9]
    (out, dz_out, h_out, qkv_out, mixed_out, g_out, gp_out, lse_out, w0_out, w1_out, w2_out, sums) = refs[9:21]
    (held0, held1, held2, small_all, tok, mask, hacc, facc, yb, qkv, mixed, act, slope, lse, cot) = refs[21:36]
    (load_sem, store_sem, z_send, z_recv, x_send, x_recv, s_send, s_recv) = refs[36:]
    me = Place(groups, parts)
    n = me.count
    wide, width = jnp.float32, tok.shape[1]
    count, seq = tok.shape[0], mask.shape[1]
    split = mixed.shape[2]
    heads = split // HD
    shards, held, weights = (first, w_hidden, w_project), (held0, held1, held2), (w0_out, w1_out, w2_out)
    half = width // 2
    bits_order = orders(n)
    loads, stores = [], []

    def load(src, dst):
        loads.append(pltpu.make_async_copy(src, dst, load_sem.at[len(loads)]))
        loads[-1].start()

    def store(src, dst, slot):
        return pltpu.make_async_copy(src, dst, store_sem.at[slot])

    load(first, held0.at[me.t])
    load(inputs.at[pl.ds(me.t * count, count)], tok)
    load(w_hidden, held1.at[me.t])
    load(w_project, held2.at[me.t])
    load(cot_in, cot)
    me.enter()
    mine = me.pieces(())
    turn = [(0, j) for j in range(1, groups)]
    turn += [(a, j) for j in range(1, groups) for a in (1, 2)]
    units = len(turn)
    hops, doubles, tiny = {}, {}, []
    for j in range(1, groups):
        tiny.append(send(small, small_all.at[me.t], (s_send, s_recv), j - 1, me.along(j)))
        tiny[-1].start()
    for u, (a, j) in enumerate(turn):
        hops[u] = send(shards[a].at[mine], held[a].at[(me.t,) + mine], (z_send, z_recv), u, me.along(j))
        hops[u].start()
    for u, (a, j) in enumerate(turn):
        source = (me.t + groups - j) % groups
        stores.append(store(held[a].at[source], weights[a].at[source], u))
        for stage in range(n):
            for h in range(2 if stage < n - 1 else 1):
                if stage == n - 1:
                    bit, done, cols = 0, set(range(1, n)), slice(None)
                else:
                    bit, done = bits_order[h][stage], set(bits_order[h][:stage])
                    cols = pl.ds(h * half, half)
                view = (source,) + me.pieces(done) + (slice(None), cols)
                slot = (u * n + stage) * 2 + h
                doubles[u, stage, h] = send(
                    held[a].at[view], held[a].at[view], (x_send, x_recv), slot, me.partner(bit)
                )

    def advance(u, stage):
        for h in range(2):
            if stage == 0:
                if h == 0:
                    hops[u].wait_recv()
            elif (u, stage - 1, h) in doubles:
                doubles[u, stage - 1, h].wait_recv()
        if stage == n:
            stores[u].start()
        for h in range(2):
            if (u, stage, h) in doubles:
                doubles[u, stage, h].start()

    plan = Plan()
    for u in range(units):
        for stage in range(n + 1):
            plan.add(HOP[0] + HOP[1] * u + HOP[2] * stage, (u, stage))
    for j in range(groups):
        plan.point(("start", j), 0.0, (turn.index((0, j)), n) if j else None)
        plan.point(("project", j), 1.8)
        plan.point(("attend", j), 1.7)
        plan.point(("combine", j), 1.7)
        plan.point(("combined", j), 1.0)
    plan.point(("norm", 0), 1.5)
    for j in range(groups):
        plan.point(("up", j), 0.0, (turn.index((1, j)), n) if j else None)
        plan.point(("upped", j), 1.8)
        plan.point(("down", j), 1.8, (turn.index((2, j)), n) if j else None)
        plan.point(("downed", j), 1.3)
        plan.point(("next", j), 1.3)

    def run(index, name, extra=None):
        at_point(plan, advance, groups, index, name, extra)

    def group(j):
        return (me.t + groups - j) % groups

    def weight(a, g):
        return held[a][g].reshape(width, width)

    def project(g):
        bias = small_all[g, 0:1, : 3 * split].astype(wide)

        def body(r):
            total = jnp.dot(tok[r, :], weight(0, g)[:, : 3 * split], preferred_element_type=wide)
            qkv[g, r, :] = (total + bias).astype(LOW)

        row_tiles(count, TILE, body)

    span = 128
    blocks = seq // span
    factor = SCORE * HD ** (-0.5)

    def attend(g, hook):
        def packed_row(p, carry):
            base = p * seq

            def at(lo, hi):
                return pl.ds(pl.multiple_of(base + lo, span), hi - lo)

            turned = qkv[g, at(0, seq), 2 * split :].T
            for b in range(blocks):
                lo, hi = key_window(b, blocks, span)
                here = (b * span, (b + 1) * span)
                bias = mask[p, lo:hi, here[0] : here[1]]
                scores, sums_e, mixes = [], [], []
                for h in range(heads):
                    q = qkv[g, at(*here), h * HD : (h + 1) * HD]
                    k = qkv[g, at(lo, hi), split + h * HD : split + (h + 1) * HD]
                    scores.append(matmul_t(k, q))
                for h in range(heads):
                    s = scores[h] * factor + bias
                    top = jnp.max(s, axis=0, keepdims=True)
                    e = jnp.exp2(s - top)
                    total = jnp.sum(e, axis=0, keepdims=True)
                    lse[g, p * blocks + b, h : h + 1, :] = top + jnp.log(total) * SCORE
                    sums_e.append((e.astype(LOW), total))
                for h in range(heads):
                    e, total = sums_e[h]
                    o = jnp.dot(turned[h * HD : (h + 1) * HD, lo:hi], e, preferred_element_type=wide)
                    mixes.append(o * (1.0 / total))
                mixed[g, at(*here), :] = jnp.concatenate(mixes, axis=0).T.astype(LOW)
            hook(p)
            return carry

        lax.fori_loop(0, count // seq, packed_row, 0)

    def combine(g):
        def body(r):
            hacc[r, :] = hacc[r, :] + matmul_t(mixed[g, r, :], weight(0, g)[:, 3 * split :])

        row_tiles(count, TILE, body)

    def start_sum():
        def body(r):
            hacc[r, :] = tok[r, :].astype(wide) + rows[0:1]

        row_tiles(count, TILE, body)

    def first_norm():
        def body(r):
            y, _, _ = norm_forward(hacc[r, :], rows[1:2], rows[2:3])
            yb[r, :] = y.astype(LOW)
            facc[r, :] = y + rows[5:6]

        row_tiles(count, 64, body)

    def ffn_up(g, hook):
        bias = small_all[g, 1:2, :].astype(wide)

        def body(r):
            u = jnp.dot(yb[r, :], weight(1, g), preferred_element_type=wide) + bias
            below = 0.5 + 0.5 * lax.erf(u * root_half)
            act[g, r, :] = (u * below).astype(LOW)
            bell = jnp.exp2(u * u * (-0.5 * SCORE)) * 0.3989422804014327
            slope[g, r, :] = (below + u * bell).astype(LOW)

        row_tiles(count, TILE, body, hook)

    def ffn_down(g, hook):
        def body(r):
            facc[r, :] = facc[r, :] + jnp.dot(act[g, r, :], weight(2, g), preferred_element_type=wide)

        row_tiles(count, TILE, body, hook)

    def last_norm():
        def step(i, carry):
            r = pl.ds(pl.multiple_of(i * 64, 64), 64)
            y, scaled, inverse = norm_forward(facc[r, :], rows[3:4], rows[4:5])
            tok[r, :] = y.astype(LOW)
            grad = cot[r, :].astype(wide)
            dz = norm_backward(grad, scaled, inverse, rows[3:4])
            facc[r, :] = dz
            return (
                carry[0] + fold(grad * scaled),
                carry[1] + fold(grad),
                carry[2] + fold(dz.astype(LOW).astype(wide)),
            )

        zero = jnp.zeros((8, width), wide)
        found = lax.fori_loop(0, count // 64, step, (zero, zero, zero))
        for i in range(3):
            sums[i : i + 1, :] = jnp.sum(found[i], axis=0, keepdims=True)

    small_all[me.t] = small[...]
    make_mask(mask, seg_col, seg_row)
    loads[0].wait()
    loads[1].wait()
    half_way = count // TILE // 2 - 1
    start_sum()

    def attend_stores(g, j):
        return [
            store(a.at[g], b.at[g], units + groups * i + j)
            for i, (a, b) in enumerate(((qkv, qkv_out), (mixed, mixed_out), (lse, lse_out)))
        ]

    def ffn_stores(g, j):
        return [
            store(a.at[g], b.at[g], units + groups * (3 + i) + j)
            for i, (a, b) in enumerate(((act, g_out), (slope, gp_out)))
        ]

    def attend_group(j, carry):
        @pl.when(j == 1)
        def _():
            for t in tiny:
                t.wait()

        g = group(j)
        run(j, "start")
        project(g)
        run(j, "project")
        attend(g, lambda p: run(j, "attend", p == 0))
        run(j, "combine")
        combine(g)
        for copy in attend_stores(g, j):
            copy.start()
        run(j, "combined")
        return carry

    def ffn_group(j, carry):
        g = group(j)
        run(j, "up")
        ffn_up(g, lambda i: run(j, "upped", i == half_way))
        run(j, "down")
        ffn_down(g, lambda i: run(j, "downed", i == half_way))
        for copy in ffn_stores(g, j):
            copy.start()
        run(j, "next")
        return carry

    lax.fori_loop(0, groups, attend_group, 0)
    for i in range(2, 5):
        loads[i].wait()
    first_norm()
    base = units + 5 * groups
    others = [store(hacc, h_out, base)]
    others[0].start()
    for task in plan.at["norm", 0]:
        advance(*task)
    lax.fori_loop(0, groups, ffn_group, 0)
    for _, task in plan.tasks:
        advance(*task)
    last_norm()
    others += [store(tok, out, base + 1), store(facc, dz_out, base + 2)]
    for a in range(3):
        others.append(store(held[a].at[me.t], weights[a].at[me.t], base + 3 + a))
    for copy in others[1:]:
        copy.start()
    stores += others
    for j in range(groups):
        stores += attend_stores(group(j), j) + ffn_stores(group(j), j)
    for copy in hops.values():
        copy.wait_send()
    for copy in doubles.values():
        copy.wait_send()
    for copy in stores:
        copy.wait()


def forward(shards, inputs, cotangent, small, rows, segments, groups, parts):
    n = parts.bit_length() - 1
    width, count = inputs.shape[1], cotangent.shape[0]
    split = width // groups
    shape = (2,) * n + (width // parts, width)
    packed, seq = segments.shape
    units = 3 * (groups - 1)
    anywhere, vmem = pl.BlockSpec(memory_space=pl.ANY), pl.BlockSpec(memory_space=pltpu.VMEM)
    wide = jnp.float32

    def made(*dims):
        return lambda kind, dtype: kind(dims, dtype)

    tokens, grouped = made(count, width), made(groups, count, width)
    layout = [
        (tokens, LOW),
        (tokens, wide),
        (tokens, wide),
        (made(groups, count, 3 * split), LOW),
        (made(groups, count, split), LOW),
        (grouped, LOW),
        (grouped, LOW),
        (made(groups, packed * seq // 128, 8, 128), wide),
    ] + [(made(groups, *shape), LOW)] * 3 + [(made(8, width), wide)]
    dma = pltpu.SemaphoreType.DMA
    outs = pl.pallas_call(
        functools.partial(forward_kernel, groups, parts),
        out_shape=[f(jax.ShapeDtypeStruct, dtype) for f, dtype in layout],
        in_specs=[anywhere] * 5 + [vmem] * 4,
        out_specs=[anywhere] * (len(layout) - 1) + [vmem],
        scratch_shapes=[pltpu.VMEM((groups,) + shape, LOW)] * 3
        + [
            pltpu.VMEM((groups,) + small.shape, LOW),
            pltpu.VMEM((count, width), LOW),
            pltpu.VMEM((packed, seq, seq), wide),
            pltpu.VMEM((count, width), wide),
            pltpu.VMEM((count, width), wide),
            pltpu.VMEM((count, width), LOW),
            pltpu.VMEM((groups, count, 3 * split), LOW),
            pltpu.VMEM((groups, count, split), LOW),
            pltpu.VMEM((groups, count, width), LOW),
            pltpu.VMEM((groups, count, width), LOW),
            pltpu.VMEM((groups, packed * seq // 128, 8, 128), wide),
            pltpu.VMEM((count, width), LOW),
            dma((5,)),
            dma((units + 5 * groups + 6,)),
            dma((units,)),
            dma((units,)),
            dma((units * n * 2,)),
            dma((units * n * 2,)),
            dma((groups - 1,)),
            dma((groups - 1,)),
        ],
        compiler_params=pltpu.CompilerParams(
            collective_id=2, has_side_effects=True, vmem_limit_bytes=63 << 20
        ),
        name="gather_and_forward",
    )(
        *[s.reshape(shape) for s in shards],
        inputs,
        cotangent,
        small,
        rows,
        segments[:, None, :],
        segments[:, :, None],
    )
    weights = [w.reshape(groups, width, width) for w in outs[8:11]]
    return outs[:8], weights, outs[11]


def backward_kernel(groups, parts, *refs):
    (dz_in, h_in, qkv_in, mixed_in, act_in, slope_in, lse_in, w0_in, w1_in, w2_in, inputs) = refs[:11]
    rows, seg_row, seg_col, sums = refs[11:15]
    gi_out, out0, out1, out2, vec_out = refs[15:20]
    (held0, held1, held2, landing, final) = refs[20:25]
    (w_buf, d_buf, act, slope, grad, low, low_t, row_t, du, hid, mask, qkv, mixed, lse, dmix, dqkv) = refs[25:41]
    (vec, vec_sum, vec_land) = refs[41:44]
    (load_sem, x_send, x_recv, z_send, z_recv, v_send, v_recv) = refs[44:51]
    halves = refs[51:]
    me = Place(groups, parts)
    n = me.count
    wide, width = jnp.float32, du.shape[1]
    count, seq = du.shape[0], mask.shape[1]
    split = mixed.shape[2]
    heads = split // HD
    held = (held0, held1, held2)
    half = width // 2
    bits_order = orders(n)
    turn = [(a, i) for i in range(groups) for a in (2, 1)] + [(0, i) for i in range(groups)]
    slots = list(range(2 * groups)) + [2 * groups + 1 + 2 * i for i in range(groups)]
    units = len(turn)

    def load(slot, src, dst):
        return pltpu.make_async_copy(src, dst, load_sem.at[slot])

    def group(i):
        return (me.t + 1 + i) % groups

    def load_ffn(i):
        g, s = group(i), i % 2
        pairs = ((slope_in, slope), (w2_in, d_buf), (w1_in, w_buf), (act_in, act))
        return [load(4 + 4 * i + k, a.at[g], b.at[s]) for k, (a, b) in enumerate(pairs)]

    def load_heads(i):
        g, s = group(i), i % 2
        pairs = ((w0_in, w_buf.at[(groups + i) % 2]), (qkv_in, qkv.at[s]), (mixed_in, mixed.at[s]), (lse_in, lse.at[s]))
        return [load(4 + 4 * groups + 4 * i + k, a.at[g], b) for k, (a, b) in enumerate(pairs)]

    def start(copies):
        for copy in copies:
            copy.start()

    def finish_all(copies):
        for copy in copies:
            copy.wait()

    entry = [load(0, dz_in, grad), load(1, h_in, hid)]
    start(entry)
    start(load_ffn(0))
    me.enter()
    copies, hops, tiny = {}, {}, {}

    def advance_vectors(stage):
        source = vec if stage == 0 else vec_sum.at[stage - 1]
        if stage:
            tiny[stage - 1].wait_recv()
            before = vec[...] if stage == 1 else vec_sum[stage - 2]
            vec_sum[stage - 1] = before + vec_land[stage - 1]
        peers = [me.partner(stage)] if stage < n else [me.along(j) for j in range(1, groups)]
        for k, peer in enumerate(peers):
            copy = send(source, vec_land.at[stage + k], (v_send, v_recv), stage + k, peer)
            copy.start()
            tiny[stage + k] = copy

    for u, (a, i) in enumerate(turn):
        target = group(i)
        copies[u, 0, 0] = send(
            held[a].at[(target,) + me.pieces(set(range(1, n)), 0)],
            landing.at[u],
            (x_send, x_recv),
            u * 2 * n,
            me.partner(0),
        )
        for stage in range(1, n):
            for h in range(2):
                bits = bits_order[h]
                bit, left = bits[stage - 1], set(bits[stage:])
                copies[u, stage, h] = send(
                    held[a].at[(target,) + me.pieces(left, bit) + (slice(None), pl.ds(h * half, half))],
                    halves[stage - 1].at[u, h],
                    (x_send, x_recv),
                    u * 2 * n + stage * 2 + h,
                    me.partner(bit),
                )
        if i < groups - 1:
            slot = a * (groups - 1) + i
            hops[slot] = send(
                held[a].at[(target,) + me.pieces(())], final.at[slot], (z_send, z_recv), slot, me.along(i + 1)
            )

    def advance(u, stage):
        a, i = turn[u]
        target = group(i)
        for h in range(2):
            if (u, stage - 1, h) not in copies:
                continue
            if stage == 1:
                left, cols, source = set(range(1, n)), slice(None), landing.at[u]
            else:
                left, cols = set(bits_order[h][stage - 1 :]), pl.ds(h * half, half)
                source = halves[stage - 2].at[u, h]
            copies[u, stage - 1, h].wait_recv()
            view = (target,) + me.pieces(left) + (slice(None), cols)
            add_into(held[a].at[view], source, [2] * len(left))
        if stage == n and i < groups - 1:
            hops[a * (groups - 1) + i].start()
        for h in range(2):
            if (u, stage, h) in copies:
                copies[u, stage, h].start()

    plan = Plan()
    before = [-100.0] * (n + 1)

    def made(u):
        for stage in range(n + 1):
            when = plan.now + PASS[0] * stage
            if stage:
                when = max(when, before[stage] + PASS[1], before[stage - 1] + PASS[0])
            before[stage] = when
            plan.add(when, (u, stage))

    for i in range(groups):
        plan.now += 2.8
        made(2 * i)
        plan.point(("down", i), 0.0)
        plan.point(("back", i), 2.8)
        plan.point(("backed", i), 2.8)
        plan.now += 2.8
        made(2 * i + 1)
        plan.point(("up", i), 0.0)
    plan.point(("norm", 0), 3.0)
    plan.point(("norm", 1), 2.0)
    for i in range(groups):
        plan.point(("mix", i), 1.0)
        plan.point(("attend", i), 3.0)
        plan.point(("attended", i), 3.0)
        plan.now += 2.8
        made(2 * groups + i)
        plan.point(("first", i), 0.0)
        plan.point(("finish", i), 2.2)

    def run(index, name, extra=None):
        at_point(plan, advance, groups, index, name, extra)

    def put(a, g, cols, value):
        shape = held[a].shape[1:-1] + value.shape[1:]
        held[a][(g,) + (slice(None),) * (n + 1) + (cols,)] = value.astype(LOW).reshape(shape)

    def products(a, g, left, right):
        def step(i, carry):
            cols = pl.ds(pl.multiple_of(i * TILE, TILE), TILE)
            put(a, g, cols, jnp.dot(left[...], right[:, cols], preferred_element_type=wide))
            return carry

        lax.fori_loop(0, width // TILE, step, 0)

    def flip(dst, r, value):
        dst[:, r] = value.T

    vec[...] = jnp.zeros_like(vec)
    finish_all(entry)

    def prepare(i, carry):
        r = pl.ds(pl.multiple_of(i * 128, 128), 128)
        g = grad[r, :].astype(LOW)
        low[r, :] = g
        flip(low_t, r, g)
        y, _, _ = norm_forward(hid[r, :], rows[1:2], rows[2:3])
        flip(row_t, r, y.astype(LOW))
        return carry

    lax.fori_loop(0, count // 128, prepare, 0)
    make_mask(mask, seg_col, seg_row)

    half_way = count // TILE // 2 - 1

    def ffn_group(i, outer):
        g, s = group(i), i % 2

        @pl.when(i + 1 < groups)
        def _():
            start(load_ffn(i + 1))

        @pl.when(i + 1 == groups)
        def _():
            start(load_heads(0))

        finish_all(load_ffn(i))
        products(2, g, low_t, act.at[s])
        run(i, "down")

        def back(k, carry):
            r = pl.ds(pl.multiple_of(k * TILE, TILE), TILE)
            part = matmul_t(low[r, :], d_buf[s])
            part = (part * slope[s, r, :].astype(wide)).astype(LOW)
            du[r, :] = part
            grad[r, :] = grad[r, :] + matmul_t(part, w_buf[s])
            run(i, "back", k == half_way)
            return carry + fold(part.astype(wide))

        total = lax.fori_loop(0, count // TILE, back, jnp.zeros((8, width), wide))
        vec[pl.ds(groups + g, 1), :] = jnp.sum(total, axis=0, keepdims=True)
        run(i, "backed")
        products(1, g, row_t, du)
        run(i, "up")
        return outer

    lax.fori_loop(0, groups, ffn_group, 0)
    tokens = load(2, inputs.at[pl.ds(me.t * count, count)], du)
    tokens.start()

    def norm(i, carry):
        r = pl.ds(pl.multiple_of(i * 64, 64), 64)
        _, scaled, inverse = norm_forward(hid[r, :], rows[1:2], rows[2:3])
        dy = grad[r, :]
        dh = norm_backward(dy, scaled, inverse, rows[1:2])
        dh_low = dh.astype(LOW)
        grad[r, :] = dh
        low[r, :] = dh_low
        return (carry[0] + fold(dy * scaled), carry[1] + fold(dy), carry[2] + fold(dh_low.astype(wide)))

    zero = jnp.zeros((8, width), wide)
    found = lax.fori_loop(0, count // 64, norm, (zero, zero, zero))
    for k in range(3):
        vec[2 * groups + k : 2 * groups + k + 1, :] = jnp.sum(found[k], axis=0, keepdims=True)
    vec[2 * groups + 3 : 2 * groups + 6, :] = sums[0:3, :]
    for task in plan.at["norm", 0]:
        advance(*task)
    tokens.wait()

    def turn_over(i, carry):
        r = pl.ds(pl.multiple_of(i * 128, 128), 128)
        flip(low_t, r, low[r, :])
        flip(row_t, r, du[r, :])
        return carry

    lax.fori_loop(0, count // 128, turn_over, 0)
    for task in plan.at["norm", 1]:
        advance(*task)

    span = 128
    blocks = seq // span
    scale = HD ** (-0.5)

    def heads_group(i, outer):
        g, s, ws = group(i), i % 2, (groups + i) % 2

        @pl.when(i + 1 < groups)
        def _():
            start(load_heads(i + 1))

        finish_all(load_heads(i))

        def mix(k, carry):
            r = pl.ds(pl.multiple_of(k * TILE, TILE), TILE)
            dmix[r, :] = jnp.dot(low[r, :], w_buf[ws][:, 3 * split :], preferred_element_type=wide).astype(LOW)
            return carry

        lax.fori_loop(0, count // TILE, mix, 0)
        run(i, "mix")

        def packed_row(p, carry):
            base = p * seq

            def at(lo, hi):
                return pl.ds(pl.multiple_of(base + lo, span), hi - lo)

            turned = qkv[s, at(0, seq), split : 2 * split].T
            dks = [[None] * heads for _ in range(blocks)]
            dvs = [[None] * heads for _ in range(blocks)]
            dqs = []

            def gather_sum(total, lo, h, value):
                for c in range(value.shape[0] // span):
                    piece = value[c * span : (c + 1) * span]
                    old = total[lo // span + c][h]
                    total[lo // span + c][h] = piece if old is None else old + piece

            def write(b):
                parts_b = [dqs[b]] + [x * scale for x in dks[b]] + dvs[b]
                dqkv[at(b * span, (b + 1) * span), :] = jnp.concatenate(parts_b, axis=1).astype(LOW)

            for b in range(blocks):
                lo, hi = key_window(b, blocks, span)
                here = (b * span, (b + 1) * span)
                bias = mask[p, lo:hi, here[0] : here[1]]
                work, grads = [], []
                for h in range(heads):
                    q = qkv[s, at(*here), h * HD : (h + 1) * HD]
                    k = qkv[s, at(lo, hi), split + h * HD : split + (h + 1) * HD]
                    v = qkv[s, at(lo, hi), 2 * split + h * HD : 2 * split + (h + 1) * HD]
                    do = dmix[at(*here), h * HD : (h + 1) * HD]
                    work.append((q, do, matmul_t(k, q), matmul_t(v, do)))
                for h in range(heads):
                    q, do, score, dp = work[h]
                    prob = jnp.exp2(score * (SCORE * scale) + bias - lse[s, p * blocks + b, h : h + 1, :])
                    inner = jnp.sum(prob * dp, axis=0, keepdims=True)
                    grads.append((prob.astype(LOW), (prob * (dp - inner)).astype(LOW)))
                dq = []
                for h in range(heads):
                    q, do, _, _ = work[h]
                    prob, ds = grads[h]
                    gather_sum(dvs, lo, h, jnp.dot(prob, do, preferred_element_type=wide))
                    gather_sum(dks, lo, h, jnp.dot(ds, q, preferred_element_type=wide))
                    dq.append(jnp.dot(turned[h * HD : (h + 1) * HD, lo:hi], ds, preferred_element_type=wide))
                dqs.append(jnp.concatenate(dq, axis=0).T * scale)
                if b:
                    write(b - 1)
            write(blocks - 1)
            run(i, "attend", p == 0)
            return carry

        lax.fori_loop(0, count // seq, packed_row, 0)
        run(i, "attended")

        def first_cols(k, carry):
            cols = pl.ds(pl.multiple_of(k * TILE, TILE), TILE)
            put(0, g, cols, jnp.dot(row_t[...], dqkv[:, cols], preferred_element_type=wide))
            return carry

        edge = 3 * split // TILE * TILE
        lax.fori_loop(0, edge // TILE, first_cols, 0)
        tail = jnp.concatenate(
            [
                jnp.dot(row_t[...], dqkv[:, edge:], preferred_element_type=wide),
                jnp.dot(low_t[...], mixed[s], preferred_element_type=wide),
            ],
            axis=1,
        )
        put(0, g, slice(edge, width), tail)
        run(i, "first")

        def finish(k, carry):
            r = pl.ds(pl.multiple_of(k * TILE, TILE), TILE)
            part = dqkv[r, :]
            grad[r, :] = grad[r, :] + matmul_t(part, w_buf[ws][:, : 3 * split])
            return carry + fold(part.astype(wide))

        total = lax.fori_loop(0, count // TILE, finish, jnp.zeros((8, 3 * split), wide))
        vec[pl.ds(g, 1), : 3 * split] = jnp.sum(total, axis=0, keepdims=True)
        run(i, "finish")
        return outer

    lax.fori_loop(0, groups, heads_group, 0)
    result = load(3, grad, gi_out)
    result.start()
    rest = [task for _, task in plan.tasks]
    for stage in range(n + 1):
        advance_vectors(stage)
        for task in rest[:2] if stage < n else rest:
            advance(*task)
        rest = rest[2:]
    total = vec_sum[n - 1]
    for j in range(groups - 1):
        tiny[n + j].wait_recv()
        total = total + vec_land[n + j]
    vec_out[...] = total
    for a, out in ((2, out2), (1, out1), (0, out0)):
        total = held[a][(me.t,) + me.pieces(())].astype(wide)
        for j in range(groups - 1):
            slot = a * (groups - 1) + j
            hops[slot].wait_recv()
            total = total + final[slot].astype(wide)
        out[...] = total
    for copy in list(tiny.values()) + list(copies.values()) + list(hops.values()):
        copy.wait_send()
    result.wait()


def backward(saved, weights, sums, inputs, rows, segments, groups, parts):
    n = parts.bit_length() - 1
    _, dz, hid, qkv, mixed, act, slope, lse = saved
    count, width = dz.shape
    split = width // groups
    piece = width // parts
    shape = (groups,) + (2,) * n + (piece, width)
    packed, seq = segments.shape
    units = 3 * groups
    anywhere, vmem = pl.BlockSpec(memory_space=pl.ANY), pl.BlockSpec(memory_space=pltpu.VMEM)
    wide, dma = jnp.float32, pltpu.SemaphoreType.DMA
    lines = -(-(2 * groups + 6) // 8) * 8
    return pl.pallas_call(
        functools.partial(backward_kernel, groups, parts),
        out_shape=[jax.ShapeDtypeStruct((count, width), wide)]
        + [jax.ShapeDtypeStruct((piece, width), wide)] * 3
        + [jax.ShapeDtypeStruct((lines, width), wide)],
        in_specs=[anywhere] * 11 + [vmem] * 4,
        out_specs=[anywhere] + [vmem] * 4,
        scratch_shapes=[pltpu.VMEM(shape, LOW)] * 3
        + [
            pltpu.VMEM((units,) + (2,) * (n - 1) + (piece, width), LOW),
            pltpu.VMEM((3 * (groups - 1), piece, width), LOW),
            pltpu.VMEM((2, width, width), LOW),
            pltpu.VMEM((2, width, width), LOW),
            pltpu.VMEM((2, count, width), LOW),
            pltpu.VMEM((2, count, width), LOW),
            pltpu.VMEM((count, width), wide),
            pltpu.VMEM((count, width), LOW),
            pltpu.VMEM((width, count), LOW),
            pltpu.VMEM((width, count), LOW),
            pltpu.VMEM((count, width), LOW),
            pltpu.VMEM((count, width), wide),
            pltpu.VMEM((packed, seq, seq), wide),
            pltpu.VMEM((2, count, 3 * split), LOW),
            pltpu.VMEM((2, count, split), LOW),
            pltpu.VMEM((2, count // 128, 8, 128), wide),
            pltpu.VMEM((count, split), LOW),
            pltpu.VMEM((count, 3 * split), LOW),
            pltpu.VMEM((lines, width), wide),
            pltpu.VMEM((n, lines, width), wide),
            pltpu.VMEM((n + groups - 1, lines, width), wide),
            dma((8 * groups + 4,)),
            dma((units * 2 * n,)),
            dma((units * 2 * n,)),
            dma((3 * (groups - 1),)),
            dma((3 * (groups - 1),)),
            dma((n + groups - 1,)),
            dma((n + groups - 1,)),
        ]
        + [pltpu.VMEM((units, 2) + (2,) * (n - 1 - s) + (piece, width // 2), LOW) for s in range(1, n)],
        compiler_params=pltpu.CompilerParams(
            collective_id=3, has_side_effects=True, vmem_limit_bytes=67043328
        ),
        name="backward_and_scatter",
    )(dz, hid, qkv, mixed, act, slope, lse, *weights, inputs, rows, segments[:, None, :], segments[:, :, None], sums)


def per_device_small(
    inputs,
    segments,
    w_query,
    w_key,
    w_value,
    b_query,
    b_value,
    w_output,
    b_output,
    gain_attn,
    shift_attn,
    w_hidden,
    b_hidden,
    w_project,
    b_project,
    gain_ffn,
    shift_ffn,
    cotangent,
):
    seq_len = segments.shape[1]
    share_tokens = cotangent.shape[0]
    share_rows = share_tokens // seq_len
    width = inputs.shape[1]
    groups, parts = lax.axis_size("tensor"), lax.axis_size("dp")
    place, part = lax.axis_index("tensor"), lax.axis_index("dp")
    low = jnp.bfloat16
    wide = jnp.float32

    tokens = lax.dynamic_slice_in_dim(inputs, place * share_tokens, share_tokens, 0)
    rows_segments = lax.dynamic_slice_in_dim(segments, place * share_rows, share_rows, 0)
    split = w_query.shape[1]
    small = jnp.concatenate([b_query, b_value, b_hidden]).reshape(-1, 128)
    small_rows = small.shape[0]
    small = jnp.pad(small, ((0, -small_rows % 16), (0, 0)))
    first = jnp.concatenate([w_query, w_key, w_value, w_output.T], axis=1)
    (first, w_up, w_down), small = gather([first, w_hidden, w_project], small, groups, parts)
    w_in = first[:, :, : 3 * split].reshape(groups, width, 3, split).transpose(1, 2, 0, 3)
    w_in = w_in.reshape(width, 3 * groups * split)
    w_out = first[:, :, 3 * split :].transpose(0, 2, 1).reshape(groups * split, width)
    w_up = w_up.transpose(1, 0, 2).reshape(width, -1)
    w_down = w_down.reshape(-1, width)
    small = small[:, :small_rows].reshape(groups, -1).astype(wide)
    bias_query = small[:, :split].reshape(-1)
    bias_value = small[:, split : 2 * split].reshape(-1)
    bias_hidden = small[:, 2 * split :].reshape(-1)
    full = groups * split
    head_shape = (share_rows, seq_len, full // HD, HD)

    attn_gain = gain_attn.astype(wide)
    attn_shift = shift_attn.astype(wide)
    attn_bias = b_output.astype(wide)
    ffn_gain = gain_ffn.astype(wide)
    ffn_shift = shift_ffn.astype(wide)
    ffn_bias = b_project.astype(wide)
    grad_out = cotangent.astype(wide)

    projected = jnp.dot(tokens, w_in, preferred_element_type=wide)
    queries = (projected[:, :full] + bias_query).astype(low)
    keys_in = projected[:, full : 2 * full].astype(low)
    values = (projected[:, 2 * full :] + bias_value).astype(low)
    query_heads = queries.reshape(head_shape)
    key_heads = keys_in.reshape(head_shape)
    value_heads = values.reshape(head_shape)
    mixed_heads, logsum = lax.map(attend_forward, (query_heads, key_heads, value_heads, rows_segments))
    mixed = mixed_heads.reshape(share_tokens, full)
    hidden = tokens.astype(wide) + (jnp.dot(mixed, w_out, preferred_element_type=wide) + attn_bias)
    normed, scaled, inverse = norm_forward(hidden, attn_gain, attn_shift)
    normed_low = normed.astype(low)
    hidden_pre = jnp.dot(normed_low, w_up, preferred_element_type=wide) + bias_hidden
    active, gelu_pull = jax.vjp(gelu_exact, hidden_pre)
    active_low = active.astype(low)
    block_sum = normed + (jnp.dot(active_low, w_down, preferred_element_type=wide) + ffn_bias)
    output, scaled_out, inverse_out = norm_forward(block_sum, ffn_gain, ffn_shift)
    grad_sum = norm_backward(grad_out, scaled_out, inverse_out, ffn_gain)
    grad_ffn_gain = jnp.sum(grad_out * scaled_out, axis=0)
    grad_ffn_shift = jnp.sum(grad_out, axis=0)
    grad_sum_low = grad_sum.astype(low)
    grad_ffn_bias = jnp.sum(grad_sum_low.astype(wide), axis=0)
    grad_active = times_transposed(grad_sum_low, w_down)
    grad_w_down = cross_rows(grad_sum_low, active_low)
    grad_hidden_pre = gelu_pull(grad_active)[0].astype(low)
    grad_b_hidden = jnp.sum(grad_hidden_pre.astype(wide), axis=0)
    grad_w_up = cross_rows(normed_low, grad_hidden_pre)
    grad_normed = grad_sum + times_transposed(grad_hidden_pre, w_up)
    grad_hidden = norm_backward(grad_normed, scaled, inverse, attn_gain)
    grad_hidden_low = grad_hidden.astype(low)
    grad_attn_gain = jnp.sum(grad_normed * scaled, axis=0)
    grad_attn_shift = jnp.sum(grad_normed, axis=0)
    grad_attn_bias = jnp.sum(grad_hidden_low.astype(wide), axis=0)
    grad_w_out = cross_rows(grad_hidden_low, mixed)
    grad_mixed = times_transposed(grad_hidden_low, w_out).astype(low).reshape(head_shape)
    grad_q, grad_k, grad_v = lax.map(
        attend_backward, (query_heads, key_heads, value_heads, rows_segments, logsum, grad_mixed)
    )
    grad_q = grad_q.reshape(share_tokens, full)
    grad_k = grad_k.reshape(share_tokens, full)
    grad_v = grad_v.reshape(share_tokens, full)
    grad_projected = jnp.concatenate([grad_q, grad_k, grad_v], axis=1)
    grad_w_in = cross_rows(tokens, grad_projected)
    grad_b_query = jnp.sum(grad_q.astype(wide), axis=0)
    grad_b_value = jnp.sum(grad_v.astype(wide), axis=0)
    grad_input = grad_hidden + times_transposed(grad_projected, w_in)

    def parted(grad):
        return grad.astype(low).reshape(width, groups, -1).transpose(1, 0, 2)

    first = jnp.concatenate(
        [parted(grad_w_in[:, i * full : (i + 1) * full]) for i in range(3)] + [parted(grad_w_out)], axis=2
    )
    vectors = jnp.concatenate(
        [
            jnp.stack([grad_b_query, grad_b_value]).reshape(2 * groups, split),
            grad_b_hidden.reshape(-1, split),
            jnp.stack(
                [
                    grad_attn_gain,
                    grad_attn_shift,
                    grad_attn_bias,
                    grad_ffn_gain,
                    grad_ffn_shift,
                    grad_ffn_bias,
                ]
            ).reshape(-1, split),
        ],
        axis=0,
    )
    count = vectors.size // split
    vectors = vectors.reshape(-1, 128)
    (sum_first, sum_up, sum_down, vectors) = scatter(
        [first, parted(grad_w_up), parted(grad_w_down)], vectors, groups, parts
    )
    vectors = vectors.reshape(count, split)
    bias_qv = vectors[: 2 * groups].reshape(2, groups, split // HD, HD)
    rest = vectors[2 * groups :]
    hid = bias_hidden.shape[0] // split
    bias_h = rest[:hid].reshape(groups, -1, HD)
    vec = rest[hid:].reshape(6, -1)
    piece = HD // parts
    bias_qv = lax.dynamic_slice_in_dim(bias_qv, place, 1, 1)[:, 0]
    bias_qv = lax.dynamic_slice_in_dim(bias_qv, part * piece, piece, 2)
    bias_h = lax.dynamic_slice_in_dim(bias_h, place, 1, 0)[0]
    bias_h = lax.dynamic_slice_in_dim(bias_h, part * piece, piece, 1)
    piece = width // (parts * groups)
    vec = lax.dynamic_slice_in_dim(vec, (part * groups + place) * piece, piece, 1)
    return (
        output.astype(low),
        grad_input,
        sum_first[:, :split],
        sum_first[:, split : 2 * split],
        sum_first[:, 2 * split : 3 * split],
        sum_first[:, 3 * split :].T,
        sum_up,
        sum_down.T,
        bias_qv,
        bias_h,
        vec,
    )


def per_device(
    inputs,
    segments,
    w_query,
    w_key,
    w_value,
    b_query,
    b_value,
    w_output,
    b_output,
    gain_attn,
    shift_attn,
    w_hidden,
    b_hidden,
    w_project,
    b_project,
    gain_ffn,
    shift_ffn,
    cotangent,
):

    if (inputs.shape[1] // lax.axis_size("dp")) % 16:
        return per_device_small(
            inputs, segments, w_query, w_key, w_value, b_query, b_value, w_output, b_output, gain_attn, shift_attn,
            w_hidden, b_hidden, w_project, b_project, gain_ffn, shift_ffn, cotangent,
        )
    seq_len = segments.shape[1]
    share_tokens = cotangent.shape[0]
    share_rows = share_tokens // seq_len
    width = inputs.shape[1]
    groups, parts = lax.axis_size("tensor"), lax.axis_size("dp")
    place, part = lax.axis_index("tensor"), lax.axis_index("dp")
    low, wide = jnp.bfloat16, jnp.float32
    split = w_query.shape[1]
    nothing = jnp.zeros((split,), low)
    small = jnp.concatenate([b_query, nothing, b_value, nothing, b_hidden]).reshape(2, width)
    small = jnp.pad(small, ((0, 14), (0, 0)))
    nothing = jnp.zeros((width,), low)
    rows = [b_output, gain_attn, shift_attn, gain_ffn, shift_ffn, b_project, nothing, nothing]
    rows = jnp.concatenate(rows).reshape(8, width).astype(wide)
    rows_segments = lax.dynamic_slice_in_dim(segments, place * share_rows, share_rows, 0)
    first = jnp.concatenate([w_query, w_key, w_value, w_output.T], axis=1)
    saved, weights, sums = forward(
        [first, w_hidden, w_project], inputs, cotangent, small, rows, rows_segments, groups, parts
    )
    output = saved[0]
    grad_input, sum_first, sum_up, sum_down, vectors = backward(
        saved, weights, sums, inputs, rows, rows_segments, groups, parts
    )
    bias_qv = jnp.stack([vectors[:groups, :split], vectors[:groups, 2 * split : 3 * split]])
    bias_qv = bias_qv.reshape(2, groups, split // HD, HD)
    bias_h = vectors[groups : 2 * groups].reshape(groups, -1, HD)
    vec = vectors[2 * groups : 2 * groups + 6]
    piece = HD // parts
    bias_qv = lax.dynamic_slice_in_dim(bias_qv, place, 1, 1)[:, 0]
    bias_qv = lax.dynamic_slice_in_dim(bias_qv, part * piece, piece, 2)
    bias_h = lax.dynamic_slice_in_dim(bias_h, place, 1, 0)[0]
    bias_h = lax.dynamic_slice_in_dim(bias_h, part * piece, piece, 1)
    piece = width // (parts * groups)
    vec = lax.dynamic_slice_in_dim(vec, (part * groups + place) * piece, piece, 1)
    return (
        output.astype(low),
        grad_input,
        sum_first[:, :split],
        sum_first[:, split : 2 * split],
        sum_first[:, 2 * split : 3 * split],
        sum_first[:, 3 * split :].T,
        sum_up,
        sum_down.T,
        bias_qv,
        bias_h,
        vec,
    )


def solution(mesh):
    in_specs = (
        P("dp", None),
        P("dp", None),
        P(None, "tensor"),
        P(None, "tensor"),
        P(None, "tensor"),
        P("tensor"),
        P("tensor"),
        P("tensor", None),
        P(),
        P(),
        P(),
        P(None, "tensor"),
        P("tensor"),
        P("tensor", None),
        P(),
        P(),
        P(),
        P(("dp", "tensor"), None),
    )
    out_specs = (
        P(("dp", "tensor"), None),
        P(("dp", "tensor"), None),
        P("dp", "tensor"),
        P("dp", "tensor"),
        P("dp", "tensor"),
        P("tensor", "dp"),
        P("dp", "tensor"),
        P("tensor", "dp"),
        P(None, "tensor", "dp"),
        P("tensor", "dp"),
        P(None, ("dp", "tensor")),
    )
    return jax.shard_map(
        per_device, mesh=mesh, in_specs=in_specs, out_specs=out_specs, check_vma=False
    )
```

profile of v0, /device:TPU:0, one launch (start us, length us, event | category | flops | bytes accessed | tf_op | source)
XLA Modules:
  0.0 222.8 jit_solution(4890404102130481796)
XLA Ops:
  0.6 0.0 copy-start.4
  0.7 0.0 copy-start.11
  0.7 0.0 copy-start.12
  0.7 0.0 copy-start.5
  0.7 0.0 copy-start.6
  0.7 0.0 copy-start.7
  0.7 0.0 copy-start.8
  0.7 0.0 copy-start.9
  0.7 0.0 copy-start.10
  0.7 0.0 copy-start.3
  0.7 1.4 pad_maximum_fusion
  2.1 1.5 copy.34
  3.6 0.0 copy-done.4
  3.6 0.0 copy-done.11
  3.6 0.0 copy-done.12
  3.6 0.1 concatenate.14
  3.7 0.6 pad.4.refs_5_
  4.3 0.0 copy-done.5
  4.3 0.2 dynamic-update-slice
  4.5 0.0 copy-done.6
  4.5 0.2 dynamic-update-slice.1
  4.7 0.0 copy-done.7
  4.7 0.2 dynamic-update-slice.2
  4.9 0.0 copy-done.8
  4.9 0.2 dynamic-update-slice.3
  5.1 0.0 copy-done.9
  5.1 0.2 dynamic-update-slice.4
  5.3 0.0 copy-done.10
  5.3 0.2 dynamic-update-slice.5
  5.6 0.2 dynamic-update-slice.6
  5.8 0.6 reshape.64.refs_6_.refs_11_
  6.4 0.0 copy-done.3
  6.5 0.6 broadcast_in_dim.12.refs_7_.refs_12_
  7.1 1.0 copy.35.refs_8_.refs_13_
  8.1 96.8 %gather_and_forward.1 = (bf16[1024,768]{1,0:T(8,128)(2,1)}, f32[1024,768]{1,0:T(8,128)}, f32[1024,768]{1,0:T(8,128)}, bf16[4,1024,576]{2,1,0:T(8,128)(2,1)}, bf1...) custom-call(bf16[2,2,2,96,768]{4,3,2,1,0:T(8,128)(2,1)} %bitcast.19,, ...), custom_call_target="tpu_custom_call" | custom-call | tf_op jit(solution)/shard_map/gather_and_forward/pallas_call | solution.py:789
  104.9 104.9 %backward_and_scatter.1 = (f32[1024,768]{1,0:T(8,128)}, f32[96,768]{1,0:T(8,128)}, f32[96,768]{1,0:T(8,128)}, f32[96,768]{1,0:T(8,128)}, f32[16,768]{1,0:T(8,128)}) custom-call(f32[1024,768]{1,0:T(8,128)} %get-tuple-element.29.refs_0_, f32[1024,768]{1,0:T(8,128)} %get-tuple-element.30.refs_1_, bf16[4,1024,576]{2,1,0:T(8,128)(2,1)} %get-tuple-element.31.refs_2_, ...), custom_call_target="tpu_custom_call" | custom-call | tf_op jit(solution)/shard_map/backward_and_scatter/pallas_call | solution.py:1215
  209.8 0.0 copy-start
  209.8 2.0 slice_bitcast_fusion
  211.8 0.7 copy.39
  212.5 0.7 fusion.1
  213.2 0.1 stack.9
  213.3 0.1 stack.10
  213.4 0.1 fusion
  213.5 0.6 copy.41
  214.1 0.7 slice.30
  214.8 0.1 reshape.63
  214.9 0.1 constant_dynamic-slice_fusion.1
  215.0 0.7 copy.38
  215.6 0.7 slice.31
  216.4 0.7 constant_dynamic-slice_fusion
  217.0 2.7 %copy.53 = bf16[1024,768]{1,0:T(8,128)(2,1)} copy(bf16[1024,768]{1,0:T(8,128)(2,1)} %get-tuple-element.84) | data formatting | bytes 3145728
  219.7 0.0 copy-done
  219.7 0.0 copy-start.2
  219.7 0.0 copy-start.1
  219.7 1.7 copy.54
  221.4 0.0 copy-done.2
  221.4 0.7 copy.55
  222.1 0.0 copy-done.1
  222.1 0.7 copy.56
  (6 shorter events, 0.0 us)
Async XLA Ops:
  0.6 2.9 %copy-start.4 = (bf16[768]{0:T(1024)(128)(2,1)S(1)}, bf16[768]{0:T(1024)(128)(2,1)}, u32[]{:S(2)}) copy-start(bf16[768]{0:T(1024)(128)(2,1)} %param.30) | copy-start | bytes 4612
  0.7 2.9 %copy-start.11 = (bf16[192]{0:T(256)(128)(2,1)S(1)}, bf16[192]{0:T(256)(128)(2,1)}, u32[]{:S(2)}) copy-start(bf16[192]{0:T(256)(128)(2,1)} %param.23) | copy-start | bytes 1156
  0.7 2.9 %copy-start.12 = (bf16[192]{0:T(256)(128)(2,1)S(1)}, bf16[192]{0:T(256)(128)(2,1)}, u32[]{:S(2)}) copy-start(bf16[192]{0:T(256)(128)(2,1)} %param.24) | copy-start | bytes 1156
  0.7 3.6 %copy-start.5 = (bf16[768]{0:T(1024)(128)(2,1)S(1)}, bf16[768]{0:T(1024)(128)(2,1)}, u32[]{:S(2)}) copy-start(bf16[768]{0:T(1024)(128)(2,1)} %param.26) | copy-start | bytes 4612
  0.7 3.8 %copy-start.6 = (bf16[768]{0:T(1024)(128)(2,1)S(1)}, bf16[768]{0:T(1024)(128)(2,1)}, u32[]{:S(2)}) copy-start(bf16[768]{0:T(1024)(128)(2,1)} %param.27) | copy-start | bytes 4612
  0.7 4.0 %copy-start.7 = (bf16[768]{0:T(1024)(128)(2,1)S(1)}, bf16[768]{0:T(1024)(128)(2,1)}, u32[]{:S(2)}) copy-start(bf16[768]{0:T(1024)(128)(2,1)} %param.28) | copy-start | bytes 4612
  0.7 4.2 %copy-start.8 = (bf16[768]{0:T(1024)(128)(2,1)S(1)}, bf16[768]{0:T(1024)(128)(2,1)}, u32[]{:S(2)}) copy-start(bf16[768]{0:T(1024)(128)(2,1)} %param.33) | copy-start | bytes 4612
  0.7 4.4 %copy-start.9 = (bf16[768]{0:T(1024)(128)(2,1)S(1)}, bf16[768]{0:T(1024)(128)(2,1)}, u32[]{:S(2)}) copy-start(bf16[768]{0:T(1024)(128)(2,1)} %param.34) | copy-start | bytes 4612
  0.7 4.6 %copy-start.10 = (bf16[768]{0:T(1024)(128)(2,1)S(1)}, bf16[768]{0:T(1024)(128)(2,1)}, u32[]{:S(2)}) copy-start(bf16[768]{0:T(1024)(128)(2,1)} %param.32) | copy-start | bytes 4612
  0.7 5.7 %copy-start.3 = (s32[8,512]{1,0:T(8,128)S(1)}, s32[8,512]{1,0:T(8,128)}, u32[]{:S(2)}) copy-start(s32[8,512]{1,0:T(8,128)} %param.19) | copy-start | bytes 49156
  209.8 9.9 %copy-start = (f32[1024,768]{1,0:T(8,128)S(1)}, f32[1024,768]{1,0:T(8,128)}, u32[]{:S(2)}) copy-start(f32[1024,768]{1,0:T(8,128)} %get-tuple-element.85) | copy-start | bytes 9437188
  219.7 1.7 copy-start.2
  219.7 2.4 %copy-start.1 = (f32[96,768]{1,0:T(8,128)S(1)}, f32[96,768]{1,0:T(8,128)}, u32[]{:S(2)}) copy-start(f32[96,768]{1,0:T(8,128)} %get-tuple-element.43) | copy-start | bytes 884740
where the time goes:
time: 223 us
  Pallas kernels  202 us (91%)
  local copies, waits for them, and re-layouts  18.9 us (8%)
    pallas_call x1, Pallas kernels, backward(): pl.pallas_call(functools.partial(backward_kernel, groups, parts), out_sha...  105 us
    pallas_call x1, Pallas kernels, forward(): pl.pallas_call(functools.partial(forward_kernel, groups, parts), out_shap...  96.8 us
    unnamed x37, local copies, waits for them, and re-layouts  7.76 us

commit v1 on v0

--- a/solution.py
+++ b/solution.py
@@ -476,19 +476,22 @@
     return jnp.sum(values.reshape(-1, 8, values.shape[-1]), axis=0)
 
 
-def make_mask(mask, seg_col, seg_row):
+def make_mask(mask, segments, start):
     def step(r, carry):
-        mask[r] = jnp.where(seg_col[r] == seg_row[r], 0.0, -1.0e9)
+        row = segments[pl.ds(start + r, 1), :].astype(jnp.float32)
+        col = jnp.broadcast_to(row, (8, row.shape[1])).T[:, :1]
+        mask[r] = jnp.where(col == row, 0.0, -1.0e9)
         return carry
 
     lax.fori_loop(0, mask.shape[0], step, 0)
 
 
 def forward_kernel(groups, parts, *refs):
-    (first, w_hidden, w_project, inputs, cot_in, small, rows, seg_row, seg_col) = refs[:9]
-    (out, dz_out, h_out, qkv_out, mixed_out, g_out, gp_out, lse_out, w0_out, w1_out, w2_out, sums) = refs[9:21]
-    (held0, held1, held2, small_all, tok, mask, hacc, facc, yb, qkv, mixed, act, slope, lse, cot) = refs[21:36]
-    (load_sem, store_sem, z_send, z_recv, x_send, x_recv, s_send, s_recv) = refs[36:]
+    (first, w_hidden, w_project, inputs, cot_in, segments) = refs[:6]
+    biases, vectors = refs[6:9], refs[9:15]
+    (out, dz_out, h_out, qkv_out, mixed_out, g_out, gp_out, lse_out, w0_out, w1_out, w2_out, sums) = refs[15:27]
+    (held0, held1, held2, small_all, tok, mask, hacc, facc, yb, qkv, mixed, act, slope, lse, cot, small, rows) = refs[27:44]
+    (load_sem, store_sem, z_send, z_recv, x_send, x_recv, s_send, s_recv) = refs[44:]
     me = Place(groups, parts)
     n = me.count
     wide, width = jnp.float32, tok.shape[1]
@@ -512,6 +515,18 @@
     load(w_hidden, held1.at[me.t])
     load(w_project, held2.at[me.t])
     load(cot_in, cot)
+
+    def line(ref):
+        return ref[...].astype(wide).reshape(1, -1)
+
+    gap = jnp.zeros((1, split), wide)
+    lines = [jnp.concatenate([line(biases[0]), gap, line(biases[1]), gap], axis=1), line(biases[2])]
+    lines.append(jnp.zeros((small.shape[0] - 2, width), wide))
+    small[...] = jnp.concatenate(lines, axis=0).astype(LOW)
+    for k, ref in enumerate(vectors):
+        rows[k : k + 1, :] = line(ref)
+    for k in (1, 2):
+        sums[2 + k : 3 + k, :] = rows[k : k + 1, :]
     me.enter()
     mine = me.pieces(())
     turn = [(0, j) for j in range(1, groups)]
@@ -584,7 +599,7 @@
         bias = small_all[g, 0:1, : 3 * split].astype(wide)
 
         def body(r):
-            total = jnp.dot(tok[r, :], weight(0, g)[:, : 3 * split], preferred_element_type=wide)
+            total = matmul_t(tok[r, :], weight(0, g)[: 3 * split])
             qkv[g, r, :] = (total + bias).astype(LOW)
 
         row_tiles(count, TILE, body)
@@ -629,7 +644,9 @@
 
     def combine(g):
         def body(r):
-            hacc[r, :] = hacc[r, :] + matmul_t(mixed[g, r, :], weight(0, g)[:, 3 * split :])
+            hacc[r, :] = hacc[r, :] + jnp.dot(
+                mixed[g, r, :], weight(0, g)[3 * split :], preferred_element_type=wide
+            )
 
         row_tiles(count, TILE, body)
 
@@ -685,7 +702,7 @@
             sums[i : i + 1, :] = jnp.sum(found[i], axis=0, keepdims=True)
 
     small_all[me.t] = small[...]
-    make_mask(mask, seg_col, seg_row)
+    make_mask(mask, segments, me.t * mask.shape[0])
     loads[0].wait()
     loads[1].wait()
     half_way = count // TILE // 2 - 1
@@ -761,12 +778,13 @@
         copy.wait()
 
 
-def forward(shards, inputs, cotangent, small, rows, segments, groups, parts):
+def forward(shards, inputs, cotangent, biases, vectors, segments, groups, parts):
     n = parts.bit_length() - 1
     width, count = inputs.shape[1], cotangent.shape[0]
     split = width // groups
     shape = (2,) * n + (width // parts, width)
-    packed, seq = segments.shape
+    seq = segments.shape[1]
+    packed = count // seq
     units = 3 * (groups - 1)
     anywhere, vmem = pl.BlockSpec(memory_space=pl.ANY), pl.BlockSpec(memory_space=pltpu.VMEM)
     wide = jnp.float32
@@ -789,11 +807,11 @@
     outs = pl.pallas_call(
         functools.partial(forward_kernel, groups, parts),
         out_shape=[f(jax.ShapeDtypeStruct, dtype) for f, dtype in layout],
-        in_specs=[anywhere] * 5 + [vmem] * 4,
+        in_specs=[anywhere] * 5 + [vmem] * 10,
         out_specs=[anywhere] * (len(layout) - 1) + [vmem],
         scratch_shapes=[pltpu.VMEM((groups,) + shape, LOW)] * 3
         + [
-            pltpu.VMEM((groups,) + small.shape, LOW),
+            pltpu.VMEM((groups, 16, width), LOW),
             pltpu.VMEM((count, width), LOW),
             pltpu.VMEM((packed, seq, seq), wide),
             pltpu.VMEM((count, width), wide),
@@ -805,6 +823,8 @@
             pltpu.VMEM((groups, count, width), LOW),
             pltpu.VMEM((groups, packed * seq // 128, 8, 128), wide),
             pltpu.VMEM((count, width), LOW),
+            pltpu.VMEM((16, width), LOW),
+            pltpu.VMEM((8, width), wide),
             dma((5,)),
             dma((units + 5 * groups + 6,)),
             dma((units,)),
@@ -822,10 +842,9 @@
         *[s.reshape(shape) for s in shards],
         inputs,
         cotangent,
-        small,
-        rows,
-        segments[:, None, :],
-        segments[:, :, None],
+        segments,
+        *biases,
+        *vectors,
     )
     weights = [w.reshape(groups, width, width) for w in outs[8:11]]
     return outs[:8], weights, outs[11]
@@ -833,13 +852,13 @@
 
 def backward_kernel(groups, parts, *refs):
     (dz_in, h_in, qkv_in, mixed_in, act_in, slope_in, lse_in, w0_in, w1_in, w2_in, inputs) = refs[:11]
-    rows, seg_row, seg_col, sums = refs[11:15]
-    gi_out, out0, out1, out2, vec_out = refs[15:20]
-    (held0, held1, held2, landing, final) = refs[20:25]
-    (w_buf, d_buf, act, slope, grad, low, low_t, row_t, du, hid, mask, qkv, mixed, lse, dmix, dqkv) = refs[25:41]
-    (vec, vec_sum, vec_land) = refs[41:44]
-    (load_sem, x_send, x_recv, z_send, z_recv, v_send, v_recv) = refs[44:51]
-    halves = refs[51:]
+    segments, sums = refs[11:13]
+    gi_out, out0, out1, out2, vec_out = refs[13:18]
+    (held0, held1, held2, landing, final) = refs[18:23]
+    (w_buf, d_buf, act, slope, grad, low, low_t, row_t, du, hid, mask, qkv, mixed, lse, dmix, dqkv) = refs[23:39]
+    (vec, vec_sum, vec_land) = refs[39:42]
+    (load_sem, x_send, x_recv, z_send, z_recv, v_send, v_recv) = refs[42:49]
+    halves = refs[49:]
     me = Place(groups, parts)
     n = me.count
     wide, width = jnp.float32, du.shape[1]
@@ -998,12 +1017,12 @@
         g = grad[r, :].astype(LOW)
         low[r, :] = g
         flip(low_t, r, g)
-        y, _, _ = norm_forward(hid[r, :], rows[1:2], rows[2:3])
+        y, _, _ = norm_forward(hid[r, :], sums[3:4], sums[4:5])
         flip(row_t, r, y.astype(LOW))
         return carry
 
     lax.fori_loop(0, count // 128, prepare, 0)
-    make_mask(mask, seg_col, seg_row)
+    make_mask(mask, segments, me.t * mask.shape[0])
 
     half_way = count // TILE // 2 - 1
 
@@ -1044,9 +1063,9 @@
 
     def norm(i, carry):
         r = pl.ds(pl.multiple_of(i * 64, 64), 64)
-        _, scaled, inverse = norm_forward(hid[r, :], rows[1:2], rows[2:3])
+        _, scaled, inverse = norm_forward(hid[r, :], sums[3:4], sums[4:5])
         dy = grad[r, :]
-        dh = norm_backward(dy, scaled, inverse, rows[1:2])
+        dh = norm_backward(dy, scaled, inverse, sums[3:4])
         dh_low = dh.astype(LOW)
         grad[r, :] = dh
         low[r, :] = dh_low
@@ -1086,7 +1105,7 @@
 
         def mix(k, carry):
             r = pl.ds(pl.multiple_of(k * TILE, TILE), TILE)
-            dmix[r, :] = jnp.dot(low[r, :], w_buf[ws][:, 3 * split :], preferred_element_type=wide).astype(LOW)
+            dmix[r, :] = matmul_t(low[r, :], w_buf[ws, 3 * split :, :]).astype(LOW)
             return carry
 
         lax.fori_loop(0, count // TILE, mix, 0)
@@ -1166,7 +1185,7 @@
         def finish(k, carry):
             r = pl.ds(pl.multiple_of(k * TILE, TILE), TILE)
             part = dqkv[r, :]
-            grad[r, :] = grad[r, :] + matmul_t(part, w_buf[ws][:, : 3 * split])
+            grad[r, :] = grad[r, :] + jnp.dot(part, w_buf[ws, : 3 * split, :], preferred_element_type=wide)
             return carry + fold(part.astype(wide))
 
         total = lax.fori_loop(0, count // TILE, finish, jnp.zeros((8, 3 * split), wide))
@@ -1200,14 +1219,15 @@
     result.wait()
 
 
-def backward(saved, weights, sums, inputs, rows, segments, groups, parts):
+def backward(saved, weights, sums, inputs, segments, groups, parts):
     n = parts.bit_length() - 1
     _, dz, hid, qkv, mixed, act, slope, lse = saved
     count, width = dz.shape
     split = width // groups
     piece = width // parts
     shape = (groups,) + (2,) * n + (piece, width)
-    packed, seq = segments.shape
+    seq = segments.shape[1]
+    packed = count // seq
     units = 3 * groups
     anywhere, vmem = pl.BlockSpec(memory_space=pl.ANY), pl.BlockSpec(memory_space=pltpu.VMEM)
     wide, dma = jnp.float32, pltpu.SemaphoreType.DMA
@@ -1217,7 +1237,7 @@
         out_shape=[jax.ShapeDtypeStruct((count, width), wide)]
         + [jax.ShapeDtypeStruct((piece, width), wide)] * 3
         + [jax.ShapeDtypeStruct((lines, width), wide)],
-        in_specs=[anywhere] * 11 + [vmem] * 4,
+        in_specs=[anywhere] * 11 + [vmem] * 2,
         out_specs=[anywhere] + [vmem] * 4,
         scratch_shapes=[pltpu.VMEM(shape, LOW)] * 3
         + [
@@ -1255,7 +1275,72 @@
             collective_id=3, has_side_effects=True, vmem_limit_bytes=67043328
         ),
         name="backward_and_scatter",
-    )(dz, hid, qkv, mixed, act, slope, lse, *weights, inputs, rows, segments[:, None, :], segments[:, :, None], sums)
+    )(dz, hid, qkv, mixed, act, slope, lse, *weights, inputs, segments, sums)
+
+
+def pick(values, size, index):
+    total = jnp.zeros((values.shape[0], size), values.dtype)
+    for k in range(values.shape[1] // size):
+        total = jnp.where(index == k, values[:, k * size : (k + 1) * size], total)
+    return total
+
+
+def outputs_kernel(groups, parts, *refs):
+    out_in, gi_in, first, up, down, vec = refs[:6]
+    out, gi, g_query, g_key, g_value, g_output, g_hidden, g_project, bias_qv, bias_h, vectors = refs[6:17]
+    held_out, held_gi, load_sem, store_sem = refs[17:]
+    t, d = lax.axis_index("tensor"), lax.axis_index("dp")
+    count, width = held_gi.shape
+    split, piece = width // groups, HD // parts
+    size = count // 4
+    loads, stores = [], []
+    for k in range(4):
+        r = pl.ds(k * size, size)
+        for a, b, c in ((gi_in, held_gi, gi), (out_in, held_out, out)):
+            loads.append(pltpu.make_async_copy(a.at[r], b.at[r], load_sem.at[len(loads)]))
+            stores.append(pltpu.make_async_copy(b.at[r], c.at[r], store_sem.at[len(stores)]))
+            loads[-1].start()
+    for k, target in enumerate((g_query, g_key, g_value)):
+        target[...] = first[:, k * split : (k + 1) * split]
+    g_output[...] = first[:, 3 * split :].T
+    g_hidden[...] = up[...]
+    g_project[...] = down[...]
+    for a, b in zip(loads, stores):
+        a.wait()
+        b.start()
+    own, hidden = vec[pl.ds(t, 1), :], vec[pl.ds(groups + t, 1), :]
+    heads = split // HD
+    pieces = [own[:, k * HD : (k + 1) * HD] for k in range(heads)]
+    pieces += [own[:, 2 * split + k * HD : 2 * split + (k + 1) * HD] for k in range(heads)]
+    pieces += [hidden[:, k * HD : (k + 1) * HD] for k in range(width // HD)]
+    found = pick(jnp.concatenate(pieces, axis=0), piece, d)
+    for h in range(heads):
+        bias_qv[h] = jnp.concatenate([found[h : h + 1], found[heads + h : heads + h + 1]], axis=0)
+    bias_h[...] = found[2 * heads :].T
+    vectors[...] = pick(vec[2 * groups : 2 * groups + 6, :], width // (parts * groups), d * groups + t)
+    for b in stores:
+        b.wait()
+
+
+def finish_outputs(output, grad_input, first, up, down, vec, groups, parts):
+    (count, width), (piece, _) = grad_input.shape, first.shape
+    split, wide = width // groups, jnp.float32
+    shapes = [(count, width)] + [(piece, split)] * 3 + [(split, piece), (piece, width), (piece, width)]
+    shapes += [(split // HD, 2, HD // parts), (HD // parts, width // HD), (6, width // (parts * groups))]
+    anywhere, vmem = pl.BlockSpec(memory_space=pl.ANY), pl.BlockSpec(memory_space=pltpu.VMEM)
+    return pl.pallas_call(
+        functools.partial(outputs_kernel, groups, parts),
+        out_shape=[jax.ShapeDtypeStruct((count, width), LOW)] + [jax.ShapeDtypeStruct(s, wide) for s in shapes],
+        in_specs=[anywhere] * 2 + [vmem] * 4,
+        out_specs=[anywhere] * 2 + [vmem] * 9,
+        scratch_shapes=[
+            pltpu.VMEM((count, width), LOW),
+            pltpu.VMEM((count, width), wide),
+            pltpu.SemaphoreType.DMA((8,)),
+            pltpu.SemaphoreType.DMA((8,)),
+        ],
+        name="outputs",
+    )(output, grad_input, first, up, down, vec)
 
 
 def per_device_small(
@@ -1438,59 +1523,24 @@
     shift_ffn,
     cotangent,
 ):
-
     if (inputs.shape[1] // lax.axis_size("dp")) % 16:
         return per_device_small(
             inputs, segments, w_query, w_key, w_value, b_query, b_value, w_output, b_output, gain_attn, shift_attn,
             w_hidden, b_hidden, w_project, b_project, gain_ffn, shift_ffn, cotangent,
         )
-    seq_len = segments.shape[1]
-    share_tokens = cotangent.shape[0]
-    share_rows = share_tokens // seq_len
-    width = inputs.shape[1]
+    width, split = w_query.shape
     groups, parts = lax.axis_size("tensor"), lax.axis_size("dp")
-    place, part = lax.axis_index("tensor"), lax.axis_index("dp")
-    low, wide = jnp.bfloat16, jnp.float32
-    split = w_query.shape[1]
-    nothing = jnp.zeros((split,), low)
-    small = jnp.concatenate([b_query, nothing, b_value, nothing, b_hidden]).reshape(2, width)
-    small = jnp.pad(small, ((0, 14), (0, 0)))
-    nothing = jnp.zeros((width,), low)
-    rows = [b_output, gain_attn, shift_attn, gain_ffn, shift_ffn, b_project, nothing, nothing]
-    rows = jnp.concatenate(rows).reshape(8, width).astype(wide)
-    rows_segments = lax.dynamic_slice_in_dim(segments, place * share_rows, share_rows, 0)
-    first = jnp.concatenate([w_query, w_key, w_value, w_output.T], axis=1)
+    biases = [b_query, b_value, b_hidden]
+    shared = [b_output, gain_attn, shift_attn, gain_ffn, shift_ffn, b_project]
+    first = jnp.concatenate([w_query.T, w_key.T, w_value.T, w_output], axis=0)
     saved, weights, sums = forward(
-        [first, w_hidden, w_project], inputs, cotangent, small, rows, rows_segments, groups, parts
-    )
-    output = saved[0]
+        [first, w_hidden, w_project], inputs, cotangent, biases, shared, segments, groups, parts
+    )
     grad_input, sum_first, sum_up, sum_down, vectors = backward(
-        saved, weights, sums, inputs, rows, rows_segments, groups, parts
-    )
-    bias_qv = jnp.stack([vectors[:groups, :split], vectors[:groups, 2 * split : 3 * split]])
-    bias_qv = bias_qv.reshape(2, groups, split // HD, HD)
-    bias_h = vectors[groups : 2 * groups].reshape(groups, -1, HD)
-    vec = vectors[2 * groups : 2 * groups + 6]
-    piece = HD // parts
-    bias_qv = lax.dynamic_slice_in_dim(bias_qv, place, 1, 1)[:, 0]
-    bias_qv = lax.dynamic_slice_in_dim(bias_qv, part * piece, piece, 2)
-    bias_h = lax.dynamic_slice_in_dim(bias_h, place, 1, 0)[0]
-    bias_h = lax.dynamic_slice_in_dim(bias_h, part * piece, piece, 1)
-    piece = width // (parts * groups)
-    vec = lax.dynamic_slice_in_dim(vec, (part * groups + place) * piece, piece, 1)
-    return (
-        output.astype(low),
-        grad_input,
-        sum_first[:, :split],
-        sum_first[:, split : 2 * split],
-        sum_first[:, 2 * split : 3 * split],
-        sum_first[:, 3 * split :].T,
-        sum_up,
-        sum_down.T,
-        bias_qv,
-        bias_h,
-        vec,
-    )
+        saved, weights, sums, inputs, segments, groups, parts
+    )
+    found = finish_outputs(saved[0], grad_input, sum_first, sum_up, sum_down, vectors, groups, parts)
+    return (*found[:7], found[7].T, found[8].transpose(1, 0, 2), found[9].T, found[10])
 
 
 def solution(mesh):

time: 223 us -> 209 us (0.937)
  local copies, waits for them, and re-layouts: 18.9 us -> 0 us
  Pallas kernels: 202 us -> 206 us
    unnamed x37 -> x0, local copies, waits for them, and re-layouts: 7.76 us -> none
    pallas_call x0 -> x1, Pallas kernels: none -> 7.4 us  [finish_outputs(): pl.pallas_call(functools.partial(outputs_kernel, groups, parts), out_shap...]
where the time goes in v1:
time: 209 us
  Pallas kernels  206 us (99%)
  other arithmetic  2.32 us (1%)
    pallas_call x1, Pallas kernels, backward(): pl.pallas_call(functools.partial(backward_kernel, groups, parts), out_sha...  103 us
    pallas_call x1, Pallas kernels, forward(): pl.pallas_call(functools.partial(forward_kernel, groups, parts), out_shap...  95.8 us
    pallas_call x1, Pallas kernels, finish_outputs(): pl.pallas_call(functools.partial(outputs_kernel, groups, parts), out_shap...  7.4 us

profile of v1, /device:TPU:0, one launch (start us, length us, event | category | flops | bytes accessed | tf_op | source)
XLA Modules:
  0.0 209.0 jit_solution(17186717595891787114)
XLA Ops:
  0.6 2.3 %pad_maximum_fusion = bf16[768,768]{1,0:T(8,128)(2,1)} fusion(bf16[192,768]{1,0:T(8,128)(2,1)} %param.25, bf16[192,768]{1,0:T(8,128)(2,1)} %bitcast.18, bf16[192,768]{1,0:T(8,128)(2,1)} %bitcast.19, bf16[192,768]{1,0:T(8,128)(2,1)} %bitcast.20), kind=kLoop, calls=%fused_computation | loop fusion | flops 4718592 | bytes 2359296 | tf_op jit(solution)/shard_map/concatenate | solution.py:1535
  3.0 95.8 %gather_and_forward.1 = (bf16[1024,768]{1,0:T(8,128)(2,1)}, f32[1024,768]{1,0:T(8,128)}, f32[1024,768]{1,0:T(8,128)}, bf16[4,1024,576]{2,1,0:T(8,128)(2,1)}, bf1...) custom-call(bf16[2,2,2,96,768]{4,3,2,1,0:T(8,128)(2,1)} %bitcast.12,, ...), custom_call_target="tpu_custom_call" | custom-call | tf_op jit(solution)/shard_map/gather_and_forward/pallas_call | solution.py:807
  98.7 102.9 %backward_and_scatter.1 = (f32[1024,768]{1,0:T(8,128)}, f32[96,768]{1,0:T(8,128)}, f32[96,768]{1,0:T(8,128)}, f32[96,768]{1,0:T(8,128)}, f32[16,768]{1,0:T(8,128)}) custom-call(f32[1024,768]{1,0:T(8,128)} %get-tuple-element.40.refs_0_, f32[1024,768]{1,0:T(8,128)} %get-tuple-element.41.refs_1_, bf16[4,1024,576]{2,1,0:T(8,128)(2,1)} %get-tuple-element.42.refs_2_, ...), custom_call_target="tpu_custom_call" | custom-call | tf_op jit(solution)/shard_map/backward_and_scatter/pallas_call | solution.py:1235
  201.6 7.4 %outputs.1 = (bf16[1024,768]{1,0:T(8,128)(2,1)}, f32[1024,768]{1,0:T(8,128)}, f32[96,192]{1,0:T(8,128)}, f32[96,192]{1,0:T(8,128)}, f32[96,192]{1,0:T(8,128)}, /...) custom-call(bf16[1024,768]{1,0:T(8,128)(2,1)} %get-tuple-element.39., ...), custom_call_target="tpu_custom_call" | custom-call | tf_op jit(solution)/shard_map/outputs/pallas_call | solution.py:1331

commit v2 on v1

--- a/solution.py
+++ b/solution.py
@@ -529,8 +529,9 @@
         sums[2 + k : 3 + k, :] = rows[k : k + 1, :]
     me.enter()
     mine = me.pieces(())
-    turn = [(0, j) for j in range(1, groups)]
-    turn += [(a, j) for j in range(1, groups) for a in (1, 2)]
+    away = [0, 1] + list(range(groups - 1, 1, -1))
+    turn = [(0, j) for j in away[1:]]
+    turn += [(a, j) for j in away[1:] for a in (1, 2)]
     units = len(turn)
     hops, doubles, tiny = {}, {}, []
     for j in range(1, groups):
@@ -573,16 +574,16 @@
         for stage in range(n + 1):
             plan.add(HOP[0] + HOP[1] * u + HOP[2] * stage, (u, stage))
     for j in range(groups):
-        plan.point(("start", j), 0.0, (turn.index((0, j)), n) if j else None)
+        plan.point(("start", j), 0.0, (turn.index((0, away[j])), n) if j else None)
         plan.point(("project", j), 1.8)
         plan.point(("attend", j), 1.7)
         plan.point(("combine", j), 1.7)
         plan.point(("combined", j), 1.0)
     plan.point(("norm", 0), 1.5)
     for j in range(groups):
-        plan.point(("up", j), 0.0, (turn.index((1, j)), n) if j else None)
+        plan.point(("up", j), 0.0, (turn.index((1, away[j])), n) if j else None)
         plan.point(("upped", j), 1.8)
-        plan.point(("down", j), 1.8, (turn.index((2, j)), n) if j else None)
+        plan.point(("down", j), 1.8, (turn.index((2, away[j])), n) if j else None)
         plan.point(("downed", j), 1.3)
         plan.point(("next", j), 1.3)
 
@@ -590,7 +591,7 @@
         at_point(plan, advance, groups, index, name, extra)
 
     def group(j):
-        return (me.t + groups - j) % groups
+        return (me.t + groups - jnp.where(j <= 1, j, groups + 1 - j)) % groups
 
     def weight(a, g):
         return held[a][g].reshape(width, width)

time: 209 us -> 206 us (0.986)
  Pallas kernels: 206 us -> 203 us
    pallas_call x1, Pallas kernels: 95.8 us -> 86.4 us  [forward(): pl.pallas_call(functools.partial(forward_kernel, groups, parts), out_shap...]
    pallas_call x1, Pallas kernels: 103 us -> 109 us  [backward(): pl.pallas_call(functools.partial(backward_kernel, groups, parts), out_sha...]
where the time goes in v2:
time: 206 us
  Pallas kernels  203 us (99%)
  other arithmetic  2.32 us (1%)
    pallas_call x1, Pallas kernels, backward(): pl.pallas_call(functools.partial(backward_kernel, groups, parts), out_sha...  109 us
    pallas_call x1, Pallas kernels, forward(): pl.pallas_call(functools.partial(forward_kernel, groups, parts), out_shap...  86.4 us
    pallas_call x1, Pallas kernels, finish_outputs(): pl.pallas_call(functools.partial(outputs_kernel, groups, parts), out_shap...  7.4 us

profile of v2, /device:TPU:0, one launch (start us, length us, event | category | flops | bytes accessed | tf_op | source)
XLA Modules:
  0.0 205.7 jit_solution(13944429754798401108)
XLA Ops:
  0.6 2.3 %pad_maximum_fusion = bf16[768,768]{1,0:T(8,128)(2,1)} fusion(bf16[192,768]{1,0:T(8,128)(2,1)} %param.25, bf16[192,768]{1,0:T(8,128)(2,1)} %bitcast.18, bf16[192,768]{1,0:T(8,128)(2,1)} %bitcast.19, bf16[192,768]{1,0:T(8,128)(2,1)} %bitcast.20), kind=kLoop, calls=%fused_computation | loop fusion | flops 4718592 | bytes 2359296 | tf_op jit(solution)/shard_map/concatenate | solution.py:1536
  3.0 86.4 %gather_and_forward.1 = (bf16[1024,768]{1,0:T(8,128)(2,1)}, f32[1024,768]{1,0:T(8,128)}, f32[1024,768]{1,0:T(8,128)}, bf16[4,1024,576]{2,1,0:T(8,128)(2,1)}, bf1...) custom-call(bf16[2,2,2,96,768]{4,3,2,1,0:T(8,128)(2,1)} %bitcast.12,, ...), custom_call_target="tpu_custom_call" | custom-call | tf_op jit(solution)/shard_map/gather_and_forward/pallas_call | solution.py:808
  89.3 108.9 %backward_and_scatter.1 = (f32[1024,768]{1,0:T(8,128)}, f32[96,768]{1,0:T(8,128)}, f32[96,768]{1,0:T(8,128)}, f32[96,768]{1,0:T(8,128)}, f32[16,768]{1,0:T(8,128)}) custom-call(f32[1024,768]{1,0:T(8,128)} %get-tuple-element.40.refs_0_, f32[1024,768]{1,0:T(8,128)} %get-tuple-element.41.refs_1_, bf16[4,1024,576]{2,1,0:T(8,128)(2,1)} %get-tuple-element.42.refs_2_, ...), custom_call_target="tpu_custom_call" | custom-call | tf_op jit(solution)/shard_map/backward_and_scatter/pallas_call | solution.py:1236
  198.3 7.4 %outputs.1 = (bf16[1024,768]{1,0:T(8,128)(2,1)}, f32[1024,768]{1,0:T(8,128)}, f32[96,192]{1,0:T(8,128)}, f32[96,192]{1,0:T(8,128)}, f32[96,192]{1,0:T(8,128)}, /...) custom-call(bf16[1024,768]{1,0:T(8,128)(2,1)} %get-tuple-element.39., ...), custom_call_target="tpu_custom_call" | custom-call | tf_op jit(solution)/shard_map/outputs/pallas_call | solution.py:1332

commit v3 on v2

--- a/solution.py
+++ b/solution.py
@@ -421,7 +421,7 @@
 
 
 TILE = 256
-HOP = (10.0, 6.0, 5.0)
+HOP = (9.0, 6.0, 5.0)
 PASS = (8.0, 7.0)
 SCORE = 1.4426950408889634
 

time: 206 us -> 206 us (level)
  no operation moved by 1% of the time
where the time goes in v3:
time: 206 us
  Pallas kernels  203 us (99%)
  other arithmetic  2.32 us (1%)
    pallas_call x1, Pallas kernels, backward(): pl.pallas_call(functools.partial(backward_kernel, groups, parts), out_sha...  109 us
    pallas_call x1, Pallas kernels, forward(): pl.pallas_call(functools.partial(forward_kernel, groups, parts), out_shap...  86.4 us
    pallas_call x1, Pallas kernels, finish_outputs(): pl.pallas_call(functools.partial(outputs_kernel, groups, parts), out_shap...  7.4 us

profile of v3, /device:TPU:0, one launch (start us, length us, event | category | flops | bytes accessed | tf_op | source)
XLA Modules:
  0.0 205.7 jit_solution(13944429754798401108)
XLA Ops:
  0.6 2.3 %pad_maximum_fusion = bf16[768,768]{1,0:T(8,128)(2,1)} fusion(bf16[192,768]{1,0:T(8,128)(2,1)} %param.25, bf16[192,768]{1,0:T(8,128)(2,1)} %bitcast.18, bf16[192,768]{1,0:T(8,128)(2,1)} %bitcast.19, bf16[192,768]{1,0:T(8,128)(2,1)} %bitcast.20), kind=kLoop, calls=%fused_computation | loop fusion | flops 4718592 | bytes 2359296 | tf_op jit(solution)/shard_map/concatenate | solution.py:1536
  3.0 86.4 %gather_and_forward.1 = (bf16[1024,768]{1,0:T(8,128)(2,1)}, f32[1024,768]{1,0:T(8,128)}, f32[1024,768]{1,0:T(8,128)}, bf16[4,1024,576]{2,1,0:T(8,128)(2,1)}, bf1...) custom-call(bf16[2,2,2,96,768]{4,3,2,1,0:T(8,128)(2,1)} %bitcast.12,, ...), custom_call_target="tpu_custom_call" | custom-call | tf_op jit(solution)/shard_map/gather_and_forward/pallas_call | solution.py:808
  89.3 108.9 %backward_and_scatter.1 = (f32[1024,768]{1,0:T(8,128)}, f32[96,768]{1,0:T(8,128)}, f32[96,768]{1,0:T(8,128)}, f32[96,768]{1,0:T(8,128)}, f32[16,768]{1,0:T(8,128)}) custom-call(f32[1024,768]{1,0:T(8,128)} %get-tuple-element.40.refs_0_, f32[1024,768]{1,0:T(8,128)} %get-tuple-element.41.refs_1_, bf16[4,1024,576]{2,1,0:T(8,128)(2,1)} %get-tuple-element.42.refs_2_, ...), custom_call_target="tpu_custom_call" | custom-call | tf_op jit(solution)/shard_map/backward_and_scatter/pallas_call | solution.py:1236
  198.3 7.4 %outputs.1 = (bf16[1024,768]{1,0:T(8,128)(2,1)}, f32[1024,768]{1,0:T(8,128)}, f32[96,192]{1,0:T(8,128)}, f32[96,192]{1,0:T(8,128)}, f32[96,192]{1,0:T(8,128)}, /...) custom-call(bf16[1024,768]{1,0:T(8,128)(2,1)} %get-tuple-element.39., ...), custom_call_target="tpu_custom_call" | custom-call | tf_op jit(solution)/shard_map/outputs/pallas_call | solution.py:1332
